TPU v7x, 256 devices: a whole 4x4x8 slice. The times are simulated.
256 devices in a mesh: src: 4 (over x), space: 64 (over z, y, core).
Axes of the slice: x: 4, y: 4, z: 8, core: 2. Of those that a mesh axis runs over, the one named last changes fastest.
Arguments:
- contrast: float32 [2, 64, 256, 256], P(None, None, 'space'), may hold values from -0.4 to 0.45
- measured: float32 [4, 2, 256, 256], P('src', None, 'space'), may hold values from -7 to 7
- positions: int32 [4, 2], P('src'), may hold values from 0 to 255
Outputs:
- contrast_sources: float32 [4, 2, 64, 256, 256], P('src', None, None, 'space')
- contrast_new: float32 [2, 64, 256, 256], P(None, None, 'space')
All inputs are finite; a program needn't handle non-finite values.
Results may differ from a plain program's by a relative error of at most 0.0003.
Values sent between devices are 32-bit elements; how exact they have to be, the bound alone decides.
A program may use at most 64 MiB of HBM per device.

v0:
```python
from functools import partial
import math

import jax
import jax.numpy as jnp
from jax import lax
from jax.sharding import PartitionSpec as P

NX = 256
NY = 256
NZ = 64
OUTER = 2


WAVENUMBER = 2.0 * math.pi / 6.0
DAMPING = 0.3
SOURCE_GAP = 8.0
FLOOR_SHARE = 0.75
REAL_LOW = -0.25
REAL_HIGH = 0.35
IMAG_HIGH = 0.1
DEPTH_PATTERN = "akbn,sbnxy->sakxy"
FIRST_PATTERN = "akbn,sbznj->sazkj"
SECOND_PATTERN = "akbn,sbzxn->sazxk"


def laplace_modes(start_mode, length, total):
    mode_index = (start_mode + jnp.arange(length)).astype(jnp.float32)
    half_sine = jnp.sin(math.pi * mode_index / total)
    return 4.0 * half_sine * half_sine


def green_spectrum(depth_modes, first_modes, second_modes):
    eigen = depth_modes[:, None, None] + first_modes[None, :, None] + second_modes[None, None, :]
    wave_sq = WAVENUMBER * WAVENUMBER
    real_den = eigen - wave_sq
    imag_den = wave_sq * DAMPING
    factor = wave_sq / (real_den * real_den + imag_den * imag_den)
    return (factor * real_den, factor * imag_den)


def incident(positions, start_row, row_count):
    heights = jnp.arange(NZ).astype(jnp.float32) + SOURCE_GAP
    across = (start_row + jnp.arange(row_count)).astype(jnp.float32)
    along_y = jnp.arange(NY).astype(jnp.float32)
    source_x = positions[:, 0].astype(jnp.float32)
    source_y = positions[:, 1].astype(jnp.float32)
    offset_x = across[None, :] - source_x[:, None]
    offset_y = along_y[None, :] - source_y[:, None]
    dist_sq = (
        heights[None, :, None, None] * heights[None, :, None, None]
        + offset_x[:, None, :, None] * offset_x[:, None, :, None]
    )
    dist_sq = dist_sq + offset_y[:, None, None, :] * offset_y[:, None, None, :]
    phases = WAVENUMBER * jnp.sqrt(dist_sq)
    return (jnp.cos(phases), jnp.sin(phases))


def dft_table(length, orient, factor):
    indices = jnp.arange(length)
    turn_index = indices[:, None] * indices[None, :] % length
    angles = 2.0 * math.pi / length * turn_index.astype(jnp.float32)
    cosine = jnp.cos(angles) * factor
    sine_part = orient * jnp.sin(angles) * factor
    upper_rows = jnp.stack([cosine, sine_part], axis=1)
    bottom = jnp.stack([-sine_part, cosine], axis=1)
    return jnp.stack([upper_rows, bottom], axis=0)


def apply_table(table, fields, pattern):
    return jnp.einsum(pattern, table, fields, precision=lax.Precision.HIGHEST)


def times_green(spectrum, green_real, green_imag):
    real_part = spectrum[:, 0] * green_real - spectrum[:, 1] * green_imag
    imag_part = spectrum[:, 0] * green_imag + spectrum[:, 1] * green_real
    return jnp.stack([real_part, imag_part], axis=1)


def transform(fields, spectral, tables):
    z_forward, x_forward, y_forward, z_inverse, x_inverse, y_inverse = tables
    depth_done = apply_table(z_forward, fields, DEPTH_PATTERN)
    planes = apply_table(
        x_forward,
        lax.all_to_all(depth_done, "space", split_axis=2, concat_axis=3, tiled=True),
        FIRST_PATTERN,
    )
    spectrum = spectral(apply_table(y_forward, planes, SECOND_PATTERN))
    returned = apply_table(
        x_inverse, apply_table(y_inverse, spectrum, SECOND_PATTERN), FIRST_PATTERN
    )
    return apply_table(
        z_inverse,
        lax.all_to_all(returned, "space", split_axis=3, concat_axis=2, tiled=True),
        DEPTH_PATTERN,
    )


def descent_total(descent):
    local_sum = jnp.sum(descent * descent)
    return lax.psum(local_sum, ("src", "space"))


def bounded(numerator, power_sum, total_sources):
    floored = jnp.maximum(power_sum, FLOOR_SHARE * total_sources)
    return jnp.stack(
        [
            jnp.clip(numerator[0] / floored, REAL_LOW, REAL_HIGH),
            jnp.clip(numerator[1] / floored, 0.0, IMAG_HIGH),
        ],
        axis=0,
    )


def on_device(contrast, measured, positions):
    spaces = lax.axis_size("space")
    sources = positions.shape[0]
    row_count = contrast.shape[2]
    plane_count = NZ // spaces
    start_row = lax.axis_index("space") * row_count
    total_sources = sources * lax.axis_size("src")
    chi_real, chi_imag = (contrast[0], contrast[1])
    inc_real, inc_imag = incident(positions, start_row, row_count)
    tables = (
        dft_table(NZ, 1.0, 1.0),
        dft_table(NX, 1.0, 1.0),
        dft_table(NY, 1.0, 1.0),
        dft_table(NZ, -1.0, 1.0 / NZ),
        dft_table(NX, -1.0, 1.0 / NX),
        dft_table(NY, -1.0, 1.0 / NY),
    )
    green_real, green_imag = green_spectrum(
        laplace_modes(lax.axis_index("space") * plane_count, plane_count, NZ),
        laplace_modes(0, NX, NX),
        laplace_modes(0, NY, NY),
    )
    forward_green = partial(times_green, green_real=green_real, green_imag=green_imag)
    adjoint_green = partial(times_green, green_real=green_real, green_imag=-green_imag)
    sources_field = jnp.stack(
        [chi_real * inc_real - chi_imag * inc_imag, chi_real * inc_imag + chi_imag * inc_real],
        axis=1,
    )
    scattered = transform(sources_field, forward_green, tables)
    data_real = measured[:, 0]
    data_imag = measured[:, 1]
    data_local = jnp.sum(data_real * data_real + data_imag * data_imag)
    for outer_step in range(OUTER):
        chi_inc_real = chi_real * inc_real - chi_imag * inc_imag
        chi_inc_imag = chi_real * inc_imag + chi_imag * inc_real
        object_local = jnp.sum(chi_inc_real * chi_inc_real + chi_inc_imag * chi_inc_imag)
        data_total, object_total = lax.psum((data_local, object_local), ("src", "space"))
        data_weight = 1.0 / data_total
        object_weight = 1.0 / object_total
        total_real = inc_real + scattered[:, 0]
        total_imag = inc_imag + scattered[:, 1]
        resid_real = chi_real * total_real - chi_imag * total_imag - sources_field[:, 0]
        resid_imag = chi_real * total_imag + chi_imag * total_real - sources_field[:, 1]
        adjoint_real = -object_weight * (chi_real * resid_real + chi_imag * resid_imag)
        adjoint_imag = -object_weight * (chi_real * resid_imag - chi_imag * resid_real)
        adjoint_real = adjoint_real.at[:, 0].add(data_weight * (data_real - scattered[:, 0, 0]))
        adjoint_imag = adjoint_imag.at[:, 0].add(data_weight * (data_imag - scattered[:, 1, 0]))
        adjoint_input = jnp.stack([adjoint_real, adjoint_imag], axis=1)
        residual = jnp.stack([resid_real, resid_imag], axis=1)
        adjoint_image = transform(adjoint_input, adjoint_green, tables)
        descent = object_weight * residual + adjoint_image
        descent_early = descent_total(descent)
        descent_image = transform(descent, forward_green, tables)
        image_real = descent_image[:, 0]
        image_imag = descent_image[:, 1]
        change_real = descent[:, 0] - (chi_real * image_real - chi_imag * image_imag)
        change_imag = descent[:, 1] - (chi_real * image_imag + chi_imag * image_real)
        image_local = jnp.sum(
            image_real[:, 0] * image_real[:, 0] + image_imag[:, 0] * image_imag[:, 0]
        )
        change_local = jnp.sum(change_real * change_real + change_imag * change_imag)
        image_total, change_total = lax.psum((image_local, change_local), ("src", "space"))
        step_length = descent_early / (data_weight * image_total + object_weight * change_total)
        sources_field = sources_field + step_length * descent
        scattered = scattered + step_length * descent_image
        total_real = inc_real + scattered[:, 0]
        total_imag = inc_imag + scattered[:, 1]
        numerator_real = jnp.sum(
            sources_field[:, 0] * total_real + sources_field[:, 1] * total_imag, axis=0
        )
        numerator_imag = jnp.sum(
            sources_field[:, 1] * total_real - sources_field[:, 0] * total_imag, axis=0
        )
        power_sum = jnp.sum(total_real * total_real + total_imag * total_imag, axis=0)
        numerator = jnp.stack([numerator_real, numerator_imag], axis=0)
        numerator_all, power_all = lax.psum((numerator, power_sum), "src")
        contrast_now = bounded(numerator_all, power_all, total_sources)
        chi_real = contrast_now[0]
        chi_imag = contrast_now[1]
    return (sources_field, contrast_now)


def solution(mesh):
    placed = (P(None, None, "space", None), P("src", None, "space", None), P("src", None))
    return jax.shard_map(
        on_device,
        mesh=mesh,
        in_specs=placed,
        out_specs=(P("src", None, None, "space", None), P(None, None, "space", None)),
        check_vma=False,
    )
```

profile of v0, /device:TPU:1, one launch (start us, length us, event | category | flops | bytes accessed | tf_op | source)
XLA Modules:
  0.0 782.6 jit_solution(12502016712081461501)
XLA Ops:
  10.4 6.7 copy_cosine_fusion
  17.2 3.5 add_reduce_fusion.1
  22.7 13.8 %all-to-all-start = ((f32[1,2,64,4,256]{4,1,3,0,2:T(2,128)}), f32[1,2,64,4,256]{4,1,3,0,2:T(2,128)}, u32[]{:S(2)}, u32[]{:S(2)}) async-start(f32[1,2,64,4,256]{4,1,3,0,2:T(2,128)} %copy.363), calls=%async_computation | async-start | bytes 1048576 | tf_op jit(solution)/shard_map/all_to_all | solution.py:85
  40.9 13.1 %all-to-all-done = f32[1,2,64,4,256]{4,1,3,0,2:T(2,128)} async-done(((f32[1,2,64,4,256]{4,1,3,0,2:T(2,128)}), f32[1,2,64,4,256]{4,1,3,0,2:T(2,128)}, u32[]{:S(2)}, u32[]{:S(2)}) %all-to-all-start) | async-done | bytes 524320 | tf_op jit(solution)/shard_map/all_to_all | solution.py:85
  53.9 2.0 copy.364
  56.0 2.1 convolution_bitcast_fusion.28
  58.1 1.9 convolution_bitcast_fusion.27
  61.2 2.7 convolution_bitcast_fusion.25
  63.9 2.0 copy.367
  65.9 5.9 all-to-all-start.1
  71.9 2.0 fusion.119
  73.8 78.5 %all-reduce.2 = (f32[]{:T(128)}, f32[]{:T(128)}) all-reduce(f32[]{:T(128)} %get-tuple-element.82, f32[]{:T(128)} %get-tuple-element.133), channel_id=1, replica_groups=mesh['src'=4,'space'=64] {'src','space'}, use_global_device_ids=true, to_apply=%region_1.2 | all-reduce | flops 2 | bytes 16 | tf_op jit(solution)/shard_map/psum | solution.py:151
  157.5 7.7 add_multiply_fusion.1
  168.4 25.4 %all_to_all.40 = f32[1,2,64,4,256]{4,1,3,0,2:T(2,128)S(1)} all-to-all(f32[1,2,64,4,256]{4,1,3,0,2:T(2,128)S(1)} %copy.380), channel_id=1, replica_groups=mesh['src'=4,'space'=64] {'space'}, dimensions={2} | all-to-all | bytes 1048576 | tf_op jit(solution)/shard_map/all_to_all | solution.py:85
  195.2 1.9 convolution_bitcast_fusion.21
  198.3 1.9 convolution_bitcast_fusion.19
  201.2 6.1 all-to-all-start.3
  209.0 15.9 %all-to-all-done.3 = f32[1,2,1,256,256]{4,1,2,0,3:T(2,128)} async-done(((f32[1,2,1,256,256]{4,1,2,0,3:T(2,128)}), f32[1,2,1,256,256]{4,1,2,0,3:T(2,128)}, u32[]{:S(2)}, u32[]{:S(2)}) %all-to-all-start.3) | async-done | bytes 524320 | tf_op jit(solution)/shard_map/all_to_all | solution.py:94
  228.8 23.5 %all_to_all.41 = f32[1,2,64,4,256]{4,1,3,0,2:T(2,128)} all-to-all(f32[1,2,64,4,256]{4,1,3,0,2:T(2,128)S(1)} %copy.388), channel_id=1, replica_groups=mesh['src'=4,'space'=64] {'space'}, dimensions={2} | all-to-all | bytes 1048576 | tf_op jit(solution)/shard_map/all_to_all | solution.py:85
  252.4 2.0 copy.389
  254.4 2.1 convolution_bitcast_fusion.16
  256.5 1.9 convolution_bitcast_fusion.15
  259.7 2.7 convolution_bitcast_fusion.13
  262.3 2.0 copy.392
  264.4 5.9 all-to-all-start.5
  271.2 16.8 %all-to-all-done.5 = f32[1,2,1,256,256]{4,1,2,0,3:T(2,128)} async-done(((f32[1,2,1,256,256]{4,1,2,0,3:T(2,128)}), f32[1,2,1,256,256]{4,1,2,0,3:T(2,128)}, u32[]{:S(2)}, u32[]{:S(2)}) %all-to-all-start.5) | async-done | bytes 524320 | tf_op jit(solution)/shard_map/all_to_all | solution.py:94
  292.9 74.1 %all-reduce.1 = (f32[]{:T(128)}, f32[]{:T(128)}, f32[]{:T(128)}) all-reduce(f32[]{:T(128)} %get-tuple-element.77, f32[]{:T(128)} %fusion.95, f32[]{:T(128)} %fusion.62), channel_id=1, replica_groups=mesh['src'=4,'space'=64] {'src','space'}, use_global_device_ids=true, to_apply=%region_5.6 | all-reduce | flops 3 | bytes 24 | tf_op jit(solution)/shard_map/psum | solution.py:101
  371.8 3.2 fusion.56
  375.0 2.3 fusion.49
  378.2 42.8 %all-reduce.10.cloned.1.call-done = (f32[2,64,4,256]{3,2,1,0:T(4,128)}, f32[64,4,256]{2,1,0:T(4,128)}) async-done(((f32[2,64,4,256]{3,2,1,0:T(4,128)}, f32[64,4,256]{2,1,0:T(4,128)}), (f32[2,64,4,256]{3,2,1,0:T(4,128)}, f32[64,4,256]{2,1,0:T(4,128)})) %all-reduce.10.cloned.1.call-update) | async-done | bytes 786448 | tf_op jit(solution)/shard_map/psum | solution.py:190
  423.8 3.3 add_reduce_fusion
  428.5 77.6 %psum.101 = f32[]{:T(128)} all-reduce(f32[]{:T(128)} %add_reduce_fusion), channel_id=1, replica_groups=mesh['src'=4,'space'=64] {'src','space'}, use_global_device_ids=true, to_apply=%region_13.14 | all-reduce | flops 1 | bytes 8 | tf_op jit(solution)/shard_map/psum | solution.py:151
  506.7 4.0 add_multiply_fusion
  514.9 25.6 %all_to_all.42 = f32[1,2,64,4,256]{4,1,3,0,2:T(2,128)} all-to-all(f32[1,2,64,4,256]{4,1,3,0,2:T(2,128)S(1)} %copy.427), channel_id=1, replica_groups=mesh['src'=4,'space'=64] {'space'}, dimensions={2} | all-to-all | bytes 1048576 | tf_op jit(solution)/shard_map/all_to_all | solution.py:85
  545.9 1.9 convolution_bitcast_fusion.7
  548.8 6.1 all-to-all-start.7
  556.8 15.7 %all-to-all-done.7 = f32[1,2,1,256,256]{4,1,2,0,3:T(2,128)} async-done(((f32[1,2,1,256,256]{4,1,2,0,3:T(2,128)}), f32[1,2,1,256,256]{4,1,2,0,3:T(2,128)}, u32[]{:S(2)}, u32[]{:S(2)}) %all-to-all-start.7) | async-done | bytes 524320 | tf_op jit(solution)/shard_map/all_to_all | solution.py:94
  577.2 23.5 %all_to_all.43 = f32[1,2,64,4,256]{4,1,3,0,2:T(2,128)} all-to-all(f32[1,2,64,4,256]{4,1,3,0,2:T(2,128)S(1)} %copy.435), channel_id=1, replica_groups=mesh['src'=4,'space'=64] {'space'}, dimensions={2} | all-to-all | bytes 1048576 | tf_op jit(solution)/shard_map/all_to_all | solution.py:85
  600.7 2.0 copy.436
  602.8 2.1 convolution_bitcast_fusion.4
  604.9 1.9 convolution_bitcast_fusion.3
  608.0 1.9 convolution_bitcast_fusion.1
  610.9 5.7 all-to-all-start.9
  617.0 17.3 %all-to-all-done.9 = f32[1,2,1,256,256]{4,1,2,0,3:T(2,128)S(1)} async-done(((f32[1,2,1,256,256]{4,1,2,0,3:T(2,128)}), f32[1,2,1,256,256]{4,1,2,0,3:T(2,128)S(1)}, u32[]{:S(2)}, u32[]{:S(2)}) %all-to-all-start.9) | async-done | bytes 524320 | tf_op jit(solution)/shard_map/all_to_all | solution.py:94
  638.1 74.0 %all-reduce = (f32[]{:T(128)}, f32[]{:T(128)}, f32[]{:T(128)}) all-reduce(f32[]{:T(128)} %get-tuple-element.72, f32[]{:T(128)} %fusion.96, f32[]{:T(128)} %fusion.44), channel_id=1, replica_groups=mesh['src'=4,'space'=64] {'src','space'}, use_global_device_ids=true, to_apply=%region_15.16 | all-reduce | flops 3 | bytes 24 | tf_op jit(solution)/shard_map/psum | solution.py:101
  716.6 2.1 fusion.41
  720.8 7.3 multiply_add_fusion.1
  730.3 41.9 %all-reduce.8.cloned.1.call-done = (f32[2,64,4,256]{3,0,2,1:T(2,128)}, f32[64,4,256]{2,0,1:T(8,128)}) async-done(((f32[2,64,4,256]{3,0,2,1:T(2,128)}, f32[64,4,256]{2,0,1:T(8,128)}), (f32[2,64,4,256]{3,0,2,1:T(2,128)}, f32[64,4,256]{2,0,1:T(8,128)})) %all-reduce.8.cloned.1.call-update) | async-done | bytes 786448 | tf_op jit(solution)/shard_map/psum | solution.py:190
  (210 shorter events, 73.9 us)
Async XLA Ops:
  7.2 10.0 %copy-start.44 = (f32[2,64,4,256]{3,2,1,0:T(4,128)S(1)}, f32[2,64,4,256]{3,2,1,0:T(4,128)}, u32[]{:S(2)}) copy-start(f32[2,64,4,256]{3,2,1,0:T(4,128)} %param.11) | copy-start | bytes 1572868
  10.2 6.9 copy-start.33
  10.4 146.6 %copy-start.12 = (f32[1,64,4,256]{3,2,1,0:T(4,128)}, f32[1,64,4,256]{3,2,1,0:T(4,128)S(1)}, u32[]{:S(2)}) copy-start(f32[1,64,4,256]{3,2,1,0:T(4,128)S(1)} %sqrt_multiply_fusion.1) | copy-start | bytes 786436
  17.2 3.5 copy-start.18
  20.7 136.4 %copy-start.5 = (f32[1,64,4,256]{3,2,1,0:T(4,128)}, f32[1,64,4,256]{3,2,1,0:T(4,128)S(1)}, u32[]{:S(2)}) copy-start(f32[1,64,4,256]{3,2,1,0:T(4,128)S(1)} %get-tuple-element.83) | copy-start | bytes 786436
  20.7 136.4 %copy-start.7 = (f32[1,64,4,256]{3,2,1,0:T(4,128)}, f32[1,64,4,256]{3,2,1,0:T(4,128)S(1)}, u32[]{:S(2)}) copy-start(f32[1,64,4,256]{3,2,1,0:T(4,128)S(1)} %get-tuple-element.84) | copy-start | bytes 786436
  20.7 144.6 %copy-start.3 = (f32[1,64,4,256]{3,2,1,0:T(4,128)}, f32[1,64,4,256]{3,2,1,0:T(4,128)S(1)}, u32[]{:S(2)}) copy-start(f32[1,64,4,256]{3,2,1,0:T(4,128)S(1)} %get-tuple-element.118) | copy-start | bytes 786436
  22.7 31.3 %all-to-all-start = ((f32[1,2,64,4,256]{4,1,3,0,2:T(2,128)}), f32[1,2,64,4,256]{4,1,3,0,2:T(2,128)}, u32[]{:S(2)}, u32[]{:S(2)}) async-start(f32[1,2,64,4,256]{4,1,3,0,2:T(2,128)} %copy.363), calls=%async_computation | async-start | bytes 1048576 | tf_op jit(solution)/shard_map/all_to_all | solution.py:85
  65.9 88.7 %all-to-all-start.1 = ((f32[1,2,1,256,256]{4,1,2,0,3:T(2,128)}), f32[1,2,1,256,256]{4,1,2,0,3:T(2,128)}, u32[]{:S(2)}, u32[]{:S(2)}) async-start(f32[1,2,1,256,256]{4,1,2,0,3:T(2,128)} %copy.367), calls=%async_computation.1 | async-start | bytes 1048576 | tf_op jit(solution)/shard_map/all_to_all | solution.py:94
  156.5 1.0 copy-start.31
  157.1 9.3 %copy-start.2 = (f32[1,4,256,2,64]{2,0,1,4,3:T(1,128)}, f32[1,4,256,2,64]{2,0,1,4,3:T(1,128)S(1)}, u32[]{:S(2)}) copy-start(f32[1,4,256,2,64]{2,0,1,4,3:T(1,128)S(1)} %copy.761) | copy-start | bytes 1572868
  165.2 0.8 copy-start.24
  201.2 6.1 copy-start.25
  201.2 23.7 %all-to-all-start.3 = ((f32[1,2,1,256,256]{4,1,2,0,3:T(2,128)}), f32[1,2,1,256,256]{4,1,2,0,3:T(2,128)}, u32[]{:S(2)}, u32[]{:S(2)}) async-start(f32[1,2,1,256,256]{4,1,2,0,3:T(2,128)} %copy.384), calls=%async_computation.3 | async-start | bytes 1048576 | tf_op jit(solution)/shard_map/all_to_all | solution.py:94
  207.2 1.0 copy-start.23
  208.2 16.7 %copy-start.14 = (f32[1,64,2,64]{3,1,2,0:T(8,128)S(1)}, f32[1,64,2,64]{3,1,2,0:T(8,128)}, u32[]{:S(2)}) copy-start(f32[1,64,2,64]{3,1,2,0:T(8,128)} %get-tuple-element.128) | copy-start | bytes 98308
  208.2 16.7 %copy-start.16 = (f32[1,64,2,64]{3,1,2,0:T(8,128)S(1)}, f32[1,64,2,64]{3,1,2,0:T(8,128)}, u32[]{:S(2)}) copy-start(f32[1,64,2,64]{3,1,2,0:T(8,128)} %get-tuple-element.129) | copy-start | bytes 98308
  224.9 1.9 copy-start.38
  224.9 1.9 copy-start.40
  264.4 23.6 %all-to-all-start.5 = ((f32[1,2,1,256,256]{4,1,2,0,3:T(2,128)}), f32[1,2,1,256,256]{4,1,2,0,3:T(2,128)}, u32[]{:S(2)}, u32[]{:S(2)}) async-start(f32[1,2,1,256,256]{4,1,2,0,3:T(2,128)} %copy.392), calls=%async_computation.5 | async-start | bytes 1048576 | tf_op jit(solution)/shard_map/all_to_all | solution.py:94
  270.3 150.7 %all-reduce.10.cloned.1.call-start = ((), (), s32[]{:S(2)}) async-start(), calls=%async_computation.11 | async-start | bytes 1572864 | tf_op jit(solution)/shard_map/psum | solution.py:190
  290.3 1.0 copy-start.4
  290.3 1.0 copy-start.42
  290.3 1.1 copy-start.43
  368.9 1.3 copy-start.6
  368.9 1.3 copy-start.8
  370.2 0.8 copy-start
  371.8 3.2 copy-start.19
  422.2 0.8 copy-start.9
  423.0 0.8 copy-start.35
  510.6 0.8 copy-start.29
  510.6 1.1 copy-start.10
  548.8 6.1 copy-start.21
  548.8 23.7 %all-to-all-start.7 = ((f32[1,2,1,256,256]{4,1,2,0,3:T(2,128)}), f32[1,2,1,256,256]{4,1,2,0,3:T(2,128)}, u32[]{:S(2)}, u32[]{:S(2)}) async-start(f32[1,2,1,256,256]{4,1,2,0,3:T(2,128)} %copy.431), calls=%async_computation.7 | async-start | bytes 1048576 | tf_op jit(solution)/shard_map/all_to_all | solution.py:94
  554.8 1.0 copy-start.30
  555.8 16.7 %copy-start.15 = (f32[1,64,2,64]{3,1,2,0:T(8,128)S(1)}, f32[1,64,2,64]{3,1,2,0:T(8,128)}, u32[]{:S(2)}) copy-start(f32[1,64,2,64]{3,1,2,0:T(8,128)} %get-tuple-element.128) | copy-start | bytes 98308
  555.8 16.7 %copy-start.17 = (f32[1,64,2,64]{3,1,2,0:T(8,128)S(1)}, f32[1,64,2,64]{3,1,2,0:T(8,128)}, u32[]{:S(2)}) copy-start(f32[1,64,2,64]{3,1,2,0:T(8,128)} %get-tuple-element.129) | copy-start | bytes 98308
  572.5 1.9 copy-start.39
  572.5 1.9 copy-start.41
  610.9 23.5 %all-to-all-start.9 = ((f32[1,2,1,256,256]{4,1,2,0,3:T(2,128)}), f32[1,2,1,256,256]{4,1,2,0,3:T(2,128)S(1)}, u32[]{:S(2)}, u32[]{:S(2)}) async-start(f32[1,2,1,256,256]{4,1,2,0,3:T(2,128)} %copy.439), calls=%async_computation.9 | async-start | bytes 1048576 | tf_op jit(solution)/shard_map/all_to_all | solution.py:94
  616.6 155.6 %all-reduce.8.cloned.1.call-start = ((), (), s32[]{:S(2)}) async-start(), calls=%async_computation.10 | async-start | bytes 1572864 | tf_op jit(solution)/shard_map/psum | solution.py:190
  636.1 1.0 copy-start.11
  636.1 1.0 copy-start.28
  714.7 1.0 copy-start.1
  718.7 1.0 copy-start.37
  719.7 0.9 copy-start.13
  719.7 1.1 copy-start.32
  772.2 1.7 copy-start.45
  (9 other events, 6.4 us)
Sparse Core Ops, SparseCore 0:
  378.3 42.5 all-reduce.9
  729.5 42.6 all-reduce.7
where the time goes:
time: 790 us; the launch traced here: 783 us
  blocking collectives  402 us (51%)
  waiting for transfers between devices  163 us (21%)
  other arithmetic  58.6 us (7%)
  local copies, waits for them, and re-layouts  46.7 us (6%)
  matrix products  45.3 us (6%)
  starting transfers between devices  43.6 us (6%)
  between operations  22.6 us (3%)
    psum x2, blocking collectives, on_device(): lax.psum((data_local, object_local), ('src', 'space'))  156 us
    psum x2, blocking collectives, descent_total(): return lax.psum(local_sum, ('src', 'space'))  148 us
    all_to_all x4, blocking collectives, transform(): lax.all_to_all(depth_done, 'space', split_axis=2, concat_axis=3, tiled=True)  98.1 us
    psum x2, waiting for transfers between devices, on_device(): numerator_all, power_all = lax.psum((numerator, power_sum), 'src')  84.6 us
    all_to_all x5, waiting for transfers between devices, transform(): lax.all_to_all(returned, 'space', split_axis=3, concat_axis=2, tiled=True)  65.6 us
    dot_general x30, matrix products, apply_table(): return jnp.einsum(pattern, table, fields, precision=lax.Precision.HIGHEST)  45.3 us
    all_to_all x5, starting transfers between devices, transform(): lax.all_to_all(returned, 'space', split_axis=3, concat_axis=2, tiled=True)  29.7 us
  transfers between devices with their start and end apart: 8, of which 7 were waited for; matrix products, arithmetic and copies ran while one was open for 2% of the time, Pallas kernels for 0%

commit v1 on v0

v1 whole, which is shorter than its diff:
```python
import functools
import math

import jax
import jax.numpy as jnp
import ml_dtypes
import numpy as np
from jax import lax
from jax.experimental import pallas as pl
from jax.experimental.pallas import tpu as pltpu
from jax.sharding import PartitionSpec as P

OUTER = 2
WAVENUMBER = 2.0 * math.pi / 6.0
DAMPING = 0.3
SOURCE_GAP = 8.0
FLOOR_SHARE = 0.75
REAL_LOW = -0.25
REAL_HIGH = 0.35
IMAG_HIGH = 0.1
F32 = jnp.float32
BF16 = jnp.bfloat16
MESH = pl.DeviceIdType.MESH


def hartley(length):
    turn = np.outer(np.arange(length), np.arange(length)) % length
    angle = 2.0 * np.pi / length * turn
    return (np.cos(angle) + np.sin(angle)) / np.sqrt(length)


def high_low(table):
    high = table.astype(ml_dtypes.bfloat16)
    low = (table - high.astype(np.float64)).astype(ml_dtypes.bfloat16)
    return np.stack([high, low])


def modes(length):
    return 4.0 * np.sin(np.pi * np.arange(length) / length) ** 2


def decay_tables(depth, across):
    wave_sq = WAVENUMBER * WAVENUMBER
    trace = 2.0 + modes(depth)[:, None] + modes(across)[None, :] - wave_sq * (1.0 + 1j * DAMPING)
    root = np.sqrt(trace * trace - 4.0)
    first = (trace - root) / 2.0
    second = (trace + root) / 2.0
    small = np.where(np.abs(first) < np.abs(second), first, second)
    large = np.where(np.abs(first) < np.abs(second), second, first)
    small = 1.0 / large
    kappa = wave_sq / (large - small)
    tables = np.stack([small.real, small.imag, kappa.real, kappa.imag])
    return tables.astype(np.float32)


def cmul(a, b):
    return (a[0] * b[0] - a[1] * b[1], a[0] * b[1] + a[1] * b[0])


def cmadd(a, b, c):
    return (a[0] * b[0] - a[1] * b[1] + c[0], a[0] * b[1] + a[1] * b[0] + c[1])


def half_turn(fraction):
    angle = fraction * math.pi
    sq = angle * angle
    sine = jnp.full_like(sq, -1.0 / math.factorial(11))
    for order in (9, 7, 5, 3, 1):
        sine = sine * sq + (1.0 if order % 4 == 1 else -1.0) / math.factorial(order)
    cosine = jnp.full_like(sq, 1.0 / math.factorial(12))
    for order in (10, 8, 6, 4, 2, 0):
        cosine = cosine * sq + (1.0 if order % 4 == 0 else -1.0) / math.factorial(order)
    return sine * angle, cosine


def kernel(
    cfg,
    pos_ref, chi0_ref, meas_ref, tab_ref, hy_ref, hz_ref,
    w_ref, chi_out_ref,
    chi1_ref, e_ref, s_ref, r_ref, d_ref, v_ref, sp_ref, np_ref, np_recv,
    send1, send3, recv1, recv2, recv3, red1, red2,
    ex_send, ex_recv, red_send, red_recv, x_send, x_recv,
):
    ns, g1, g2, nz, ny, rows = cfg
    halves = ny // 128
    nx = g1 * g2 * rows
    zgroups = nz // 8
    src = lax.axis_index("src")
    space = lax.axis_index("space")
    m = lax.rem(space, g1)
    grp = space // g1
    base = grp * g1

    barrier = pltpu.get_barrier_semaphore()

    def greet_group(k, carry):
        pl.semaphore_signal(barrier, inc=1, device_id=(src, base + lax.rem(m + k, g1)), device_id_type=MESH)
        return carry

    def cross_peer(k):
        return lax.rem(src + k // g2, ns), lax.rem(grp + lax.rem(k, g2), g2) * g1 + m

    def greet_cross(k, carry):
        pl.semaphore_signal(barrier, inc=1, device_id=cross_peer(k), device_id_type=MESH)
        return carry

    lax.fori_loop(1, g1, greet_group, 0)
    lax.fori_loop(1, ns * g2, greet_cross, 0)

    def remote(src_ref, dst_ref, send_sem, recv_sem, device):
        return pltpu.make_async_remote_copy(
            src_ref=src_ref, dst_ref=dst_ref, send_sem=send_sem, recv_sem=recv_sem,
            device_id=device, device_id_type=MESH,
        )

    def take(ref, sem):
        pltpu.make_async_copy(ref, ref, sem).wait()

    def reduce_start(a, parts):
        red1[a, 0] = jnp.concatenate(parts + [jnp.zeros((8 - len(parts), 128), F32)], axis=0)

        def send(k, carry):
            remote(red1.at[a, 0], red1.at[a, k], red_send.at[a, 0], red_recv.at[a, 0],
                   (src, base + lax.rem(m + k, g1))).start()
            return carry

        lax.fori_loop(1, g1, send, 0)

    def reduce_middle(a):
        take(red1.at[a, pl.ds(1, g1 - 1)], red_recv.at[a, 0])

        def add(j, total):
            return total + red1[a, lax.rem(m - j + g1, g1)]

        red2[a, 0] = lax.fori_loop(0, g1, add, jnp.zeros((8, 128), F32), unroll=True)
        take(red1.at[a, pl.ds(1, g1 - 1)], red_send.at[a, 0])

        def send(k, carry):
            remote(red2.at[a, 0], red2.at[a, k], red_send.at[a, 1], red_recv.at[a, 1], cross_peer(k)).start()
            return carry

        lax.fori_loop(1, ns * g2, send, 0)

    def reduce_end(a):
        count = ns * g2
        take(red2.at[a, pl.ds(1, count - 1)], red_recv.at[a, 1])

        def add(j, total):
            slot = lax.rem(src - j // g2 + ns, ns) * g2 + lax.rem(grp - lax.rem(j, g2) + g2, g2)
            return total + red2[a, slot]

        total = lax.fori_loop(0, count, add, jnp.zeros((8, 128), F32), unroll=True)
        take(red2.at[a, pl.ds(1, count - 1)], red_send.at[a, 1])
        return jnp.sum(total, axis=1, keepdims=True)

    def fold(acc):
        part = acc[:, :128]
        for h in range(1, halves):
            part = part + acc[:, h * 128:(h + 1) * 128]
        return jnp.sum(part, axis=0, keepdims=True)

    def split(a):
        high = a.astype(BF16)
        return high, (a - high.astype(F32)).astype(BF16)

    def dot3(a, b):
        mm = functools.partial(jnp.dot, preferred_element_type=F32)
        return mm(a[0], b[0]) + (mm(a[1], b[0]) + mm(a[0], b[1]))

    def local(src_ref, dst_ref):
        hz = (hz_ref[0], hz_ref[1])
        hy = (hy_ref[0], hy_ref[1])
        for pair in range(rows // 2):
            block = src_ref[pl.ds(2 * pair, 2)].reshape(4 * nz, ny)
            depth_done = dot3(hz, split(block))
            done = dot3(split(depth_done), hy)
            dst_ref[pl.ds(2 * pair, 2)] = done.reshape(2, 2 * nz, ny)

    def tile(ref, lead, part, comp):
        z = pl.multiple_of(part // halves * 8, 8)
        y = pl.multiple_of(lax.rem(part, halves) * 128, 128)
        return ref.at[lead, pl.ds(comp * nz + z, 8), pl.ds(y, 128)]

    def ctable(part, which):
        z = pl.multiple_of(part // halves * 8, 8)
        y = pl.multiple_of(lax.rem(part, halves) * 128, 128)
        return tuple(tab_ref[2 * which + c, pl.ds(z, 8), pl.ds(y, 128)] for c in range(2))

    def spectral(lead, part):
        return (tile(sp_ref, lead, part, 0)[...], tile(sp_ref, lead, part, 1)[...])

    def sweep_out(t):
        def summarise(part):
            root = ctable(part, 0)
            rowv = [spectral(i, part) for i in range(rows)]
            ahead = rowv[0]
            for i in range(1, rows):
                ahead = cmadd(ahead, root, rowv[i])
            behind = rowv[rows - 1]
            for i in range(rows - 2, -1, -1):
                behind = cmadd(behind, root, rowv[i])
            return ahead + behind

        def step(k, carry):
            peer = lax.rem(m + k, g1)
            vals = summarise(peer)
            for c in range(4):
                send1[peer, c] = vals[c]
            remote(send1.at[peer], recv1.at[t, k], ex_send.at[t, 0], ex_recv.at[t, 0], (src, base + peer)).start()
            return carry

        lax.fori_loop(1, g1, step, 0)
        vals = summarise(m)
        for c in range(4):
            recv1[t, 0, c] = vals[c]

    def power(value, doublings):
        for _ in range(doublings):
            value = cmul(value, value)
        return value

    def own_root():
        return ctable(m, 0)

    def middle_out(t):
        take(recv1.at[t, pl.ds(1, g1 - 1)], ex_recv.at[t, 0])
        block_root = power(own_root(), int(math.log2(rows)))

        def gather(j, carry):
            ahead, behind = carry
            slot_a = lax.rem(m - j + g1, g1)
            slot_b = lax.rem(m - (g1 - 1 - j) + g1, g1)
            ahead = cmadd(ahead, block_root, (recv1[t, slot_a, 0], recv1[t, slot_a, 1]))
            behind = cmadd(behind, block_root, (recv1[t, slot_b, 2], recv1[t, slot_b, 3]))
            return ahead, behind

        zero = jnp.zeros((8, 128), F32)
        ahead, behind = lax.fori_loop(0, g1, gather, ((zero, zero), (zero, zero)), unroll=True)
        for c, value in enumerate(ahead + behind):
            recv2[t, 0, c] = value

        def send(k, carry):
            peer = lax.rem(grp + k, g2) * g1 + m
            remote(recv2.at[t, 0], recv2.at[t, k], ex_send.at[t, 1], ex_recv.at[t, 1], (src, peer)).start()
            return carry

        lax.fori_loop(1, g2, send, 0)
        take(recv1.at[t, pl.ds(1, g1 - 1)], ex_send.at[t, 0])

    def middle_back(t):
        block_root = power(own_root(), int(math.log2(rows)))
        group_root = power(block_root, int(math.log2(g1)))
        turn = power(group_root, int(math.log2(g2)))
        real, imag = 1.0 - turn[0], turn[1]
        norm = 1.0 / (real * real + imag * imag)
        inverse = (real * norm, imag * norm)
        take(recv2.at[t, pl.ds(1, g2 - 1)], ex_recv.at[t, 1])
        left = (recv2[t, 0, 0], recv2[t, 0, 1])
        right = (recv2[t, 0, 2], recv2[t, 0, 3])
        for k in range(g2 - 1, 0, -1):
            left = cmadd(left, group_root, (recv2[t, k, 0], recv2[t, k, 1]))
            right = cmadd(right, group_root, (recv2[t, g2 - k, 2], recv2[t, g2 - k, 3]))
        left = cmul(left, inverse)
        right = cmul(right, inverse)

        def spread(j, carry):
            left, right = carry
            back = g1 - 1 - j
            for c in range(2):
                send3[j, c] = left[c]
                send3[back, 2 + c] = right[c]
            slot_a = lax.rem(m - j + g1, g1)
            slot_b = lax.rem(m - back + g1, g1)
            left = cmadd(left, block_root, (recv1[t, slot_a, 0], recv1[t, slot_a, 1]))
            right = cmadd(right, block_root, (recv1[t, slot_b, 2], recv1[t, slot_b, 3]))
            return left, right

        lax.fori_loop(0, g1, spread, (left, right), unroll=True)

        def send(k, carry):
            peer = lax.rem(m + k, g1)
            remote(send3.at[peer], recv3.at[t, k], ex_send.at[t, 2], ex_recv.at[t, 2], (src, base + peer)).start()
            return carry

        lax.fori_loop(1, g1, send, 0)
        for c in range(4):
            recv3[t, 0, c] = send3[m, c]
        take(recv2.at[t, pl.ds(1, g2 - 1)], ex_send.at[t, 1])

    def sweep_back(t):
        take(recv3.at[t, pl.ds(1, g1 - 1)], ex_recv.at[t, 2])

        def step(k, carry):
            part = lax.rem(m - k + g1, g1)
            root = ctable(part, 0)
            kappa = ctable(part, 1)
            rowv = [spectral(i, part) for i in range(rows)]
            state = (recv3[t, k, 0], recv3[t, k, 1])
            ahead = []
            for i in range(rows):
                state = cmadd(state, root, rowv[i])
                ahead.append(state)
            state = cmul((recv3[t, k, 2], recv3[t, k, 3]), root)
            for i in range(rows - 1, -1, -1):
                total = cmul((ahead[i][0] + state[0], ahead[i][1] + state[1]), kappa)
                tile(sp_ref, i, part, 0)[...] = total[0]
                tile(sp_ref, i, part, 1)[...] = total[1]
                if i:
                    state = cmul((state[0] + rowv[i][0], state[1] + rowv[i][1]), root)
            return carry

        lax.fori_loop(0, g1, step, 0)
        take(recv3.at[t, pl.ds(1, g1 - 1)], ex_send.at[t, 2])

    def convolve(t, src_ref, dst_ref, between=()):
        hooks = list(between) + [lambda: None] * 3
        local(src_ref, sp_ref)
        hooks[0]()
        sweep_out(t)
        middle_out(t)
        hooks[1]()
        middle_back(t)
        sweep_back(t)
        hooks[2]()
        local(sp_ref, dst_ref)

    def pair(ref, x, z):
        return (ref[x, pl.ds(z, 8), :], ref[x, pl.ds(nz + z, 8), :])

    def put(ref, x, z, value):
        ref[x, pl.ds(z, 8), :] = value[0]
        ref[x, pl.ds(nz + z, 8), :] = value[1]

    def each_block(body, init):
        def outer(n, carry):
            return body(n // zgroups, pl.multiple_of(lax.rem(n, zgroups) * 8, 8), carry)

        return lax.fori_loop(0, rows * zgroups, outer, init, unroll=2)

    def square(value):
        return value[0] * value[0] + value[1] * value[1]

    zero = jnp.zeros((8, ny), F32)
    source_x = pos_ref[0, 0].astype(F32)
    source_y = pos_ref[0, 1].astype(F32)
    offset_y = lax.broadcasted_iota(jnp.int32, (8, ny), 1).astype(F32) - source_y
    offset_y_sq = offset_y * offset_y
    level = lax.broadcasted_iota(jnp.int32, (8, ny), 0).astype(F32) + SOURCE_GAP

    def begin(x, z, total):
        height = level + z.astype(F32)
        offset_x = (space * rows + x).astype(F32) - source_x
        dist = jnp.sqrt(height * height + offset_x * offset_x + offset_y_sq)
        turns = dist * (1.0 / 6.0)
        sine, cosine = half_turn(turns - jnp.floor(turns + 0.5))
        wave = (1.0 - 2.0 * sine * sine, 2.0 * sine * cosine)
        put(e_ref, x, z, wave)
        field = cmul(pair(chi0_ref, x, z), wave)
        put(w_ref, x, z, field)
        return total + square(field)

    object_part = each_block(begin, zero)
    data_part = jnp.zeros((1, ny), F32)
    for x in range(rows):
        for c in range(2):
            data_part = data_part + meas_ref[x, pl.ds(c, 1), :] * meas_ref[x, pl.ds(c, 1), :]
    data_fold = data_part[:, :128]
    for h in range(1, halves):
        data_fold = data_fold + data_part[:, h * 128:(h + 1) * 128]

    pl.semaphore_wait(barrier, (g1 - 1) + (ns * g2 - 1))
    reduce_start(0, [data_fold, fold(object_part)])
    convolve(0, w_ref, s_ref, (lambda: reduce_middle(0),))
    sums = reduce_end(0)
    data_weight = 1.0 / sums[0:1]
    object_weight = 1.0 / sums[1:2]
    chi_ref = chi0_ref
    for update in range(OUTER):
        t = 1 + 2 * update
        chi_next = chi1_ref if update < OUTER - 1 else chi_out_ref

        def residual(x, z, carry, chi_ref=chi_ref, object_weight=object_weight):
            chi = pair(chi_ref, x, z)
            e, s, w = pair(e_ref, x, z), pair(s_ref, x, z), pair(w_ref, x, z)
            field = cmul(chi, (e[0] + s[0], e[1] + s[1]))
            res = (object_weight * (field[0] - w[0]), object_weight * (field[1] - w[1]))
            put(r_ref, x, z, res)
            flipped = cmul(chi, (res[0], -res[1]))
            put(v_ref, x, z, (-flipped[0], -flipped[1]))
            return carry

        each_block(residual, 0)
        for x in range(rows):
            v_ref[x, pl.ds(0, 1), :] += data_weight * (meas_ref[x, pl.ds(0, 1), :] - s_ref[x, pl.ds(0, 1), :])
            v_ref[x, pl.ds(nz, 1), :] -= data_weight * (meas_ref[x, pl.ds(1, 1), :] - s_ref[x, pl.ds(nz, 1), :])
        convolve(t, v_ref, d_ref)

        def descend(x, z, total):
            res, image = pair(r_ref, x, z), pair(d_ref, x, z)
            d = (res[0] + image[0], res[1] - image[1])
            put(d_ref, x, z, d)
            return total + square(d)

        descent_part = each_block(descend, zero)
        convolve(t + 1, d_ref, v_ref)

        def changes(x, z, total, chi_ref=chi_ref):
            chi, d, h = pair(chi_ref, x, z), pair(d_ref, x, z), pair(v_ref, x, z)
            moved = cmul(chi, h)
            return total + square((d[0] - moved[0], d[1] - moved[1]))

        change_part = each_block(changes, zero)
        image_part = jnp.zeros((1, ny), F32)
        for x in range(rows):
            image_part = image_part + square((v_ref[x, pl.ds(0, 1), :], v_ref[x, pl.ds(nz, 1), :]))
        image_fold = image_part[:, :128]
        for h in range(1, halves):
            image_fold = image_fold + image_part[:, h * 128:(h + 1) * 128]
        a = 1 + 2 * update
        reduce_start(a, [fold(descent_part), image_fold, fold(change_part)])
        reduce_middle(a)
        sums = reduce_end(a)
        length = sums[0:1] / (data_weight * sums[1:2] + object_weight * sums[2:3])

        for k in range(1, ns + 1):
            x = lax.rem(src + k, ns)

            def advance(n, carry, x=x, length=length):
                z = pl.multiple_of(n * 8, 8)
                w, s, d, h, e = (pair(ref, x, z) for ref in (w_ref, s_ref, d_ref, v_ref, e_ref))
                w = (w[0] + length * d[0], w[1] + length * d[1])
                s = (s[0] + length * h[0], s[1] + length * h[1])
                put(w_ref, x, z, w)
                put(s_ref, x, z, s)
                u = (e[0] + s[0], e[1] + s[1])
                np_ref[x, pl.ds(z, 8), :] = w[0] * u[0] + w[1] * u[1]
                np_ref[x, pl.ds(nz + z, 8), :] = w[1] * u[0] - w[0] * u[1]
                np_ref[x, pl.ds(2 * nz + z, 8), :] = square(u)
                return carry

            lax.fori_loop(0, zgroups, advance, 0, unroll=2)
            if k < ns:
                remote(np_ref.at[x], np_recv.at[update, k], x_send.at[update, 0], x_recv.at[update, 0],
                       (x, space)).start()
        take(np_recv.at[update, pl.ds(1, ns - 1)], x_recv.at[update, 0])

        def contrast(n, total):
            z = pl.multiple_of(n * 8, 8)
            parts = [np_ref[src, pl.ds(c * nz + z, 8), :] for c in range(3)]
            for k in range(1, ns):
                parts = [parts[c] + np_recv[update, k, pl.ds(c * nz + z, 8), :] for c in range(3)]
            scale = 1.0 / jnp.maximum(parts[2], FLOOR_SHARE * ns)
            chi = (jnp.clip(parts[0] * scale, REAL_LOW, REAL_HIGH), jnp.clip(parts[1] * scale, 0.0, IMAG_HIGH))
            put(chi_next, src, z, chi)
            return total + square(chi)

        chi_part = lax.fori_loop(0, zgroups, contrast, zero, unroll=2)
        for k in range(1, ns):
            remote(chi_next.at[src], chi_next.at[src], x_send.at[update, 1], x_recv.at[update, 1],
                   (lax.rem(src + k, ns), space)).start()
        if update < OUTER - 1:
            reduce_start(a + 1, [fold(chi_part) * float(ns)])
            reduce_middle(a + 1)
            sums = reduce_end(a + 1)
            object_weight = 1.0 / sums[0:1]
        take(chi_next.at[pl.ds(0, ns - 1)], x_recv.at[update, 1])
        take(np_recv.at[update, pl.ds(1, ns - 1)], x_send.at[update, 0])
        take(chi_next.at[pl.ds(0, ns - 1)], x_send.at[update, 1])
        chi_ref = chi_next


def on_device(ns, g1, g2, contrast, measured, positions):
    _, nz, rows, ny = contrast.shape
    cfg = (ns, g1, g2, nz, ny, rows)
    transforms = 1 + 2 * OUTER
    reductions = 2 * OUTER
    chi0 = contrast.transpose(2, 0, 1, 3).reshape(rows, 2 * nz, ny)
    meas = measured[0].transpose(1, 0, 2)
    tables = decay_tables(nz, ny)
    hy = high_low(hartley(ny))
    hz = high_low(np.kron(np.eye(4), hartley(nz)))
    field = (rows, 2 * nz, ny)
    vmem = pl.BlockSpec(memory_space=pltpu.VMEM)
    w, chi = pl.pallas_call(
        functools.partial(kernel, cfg),
        out_shape=(jax.ShapeDtypeStruct(field, F32), jax.ShapeDtypeStruct(field, F32)),
        in_specs=[pl.BlockSpec(memory_space=pltpu.SMEM)] + [vmem] * 5,
        out_specs=(vmem, vmem),
        scratch_shapes=[pltpu.VMEM(field, F32)] * 7 + [
            pltpu.VMEM((rows, 3 * nz, ny), F32),
            pltpu.VMEM((OUTER, ns, 3 * nz, ny), F32),
            pltpu.VMEM((g1, 4, 8, 128), F32),
            pltpu.VMEM((g1, 4, 8, 128), F32),
            pltpu.VMEM((transforms, g1, 4, 8, 128), F32),
            pltpu.VMEM((transforms, g2, 4, 8, 128), F32),
            pltpu.VMEM((transforms, g1, 4, 8, 128), F32),
            pltpu.VMEM((reductions, g1, 8, 128), F32),
            pltpu.VMEM((reductions, ns * g2, 8, 128), F32),
            pltpu.SemaphoreType.DMA((transforms, 3)),
            pltpu.SemaphoreType.DMA((transforms, 3)),
            pltpu.SemaphoreType.DMA((reductions, 2)),
            pltpu.SemaphoreType.DMA((reductions, 2)),
            pltpu.SemaphoreType.DMA((OUTER, 2)),
            pltpu.SemaphoreType.DMA((OUTER, 2)),
        ],
        compiler_params=pltpu.CompilerParams(
            collective_id=0, has_side_effects=True, vmem_limit_bytes=40 * 1024 * 1024
        ),
    )(positions, chi0, meas, tables, hy, hz)
    sources = w.reshape(rows, 2, nz, ny).transpose(1, 2, 0, 3)[None]
    return sources, chi.reshape(rows, 2, nz, ny).transpose(1, 2, 0, 3)


def solution(mesh, g2=4):
    placed = (P(None, None, "space", None), P("src", None, "space", None), P("src", None))
    return jax.shard_map(
        functools.partial(on_device, mesh.shape["src"], mesh.shape["space"] // g2, g2),
        mesh=mesh,
        in_specs=placed,
        out_specs=(P("src", None, None, "space", None), P(None, None, "space", None)),
        check_vma=False,
    )
```

time: 790 us -> 174 us (0.22)
  blocking collectives: 402 us -> 0 us
  Pallas kernels: 0 us -> 168 us
  waiting for transfers between devices: 163 us -> 0 us
  other arithmetic: 58.6 us -> 0 us
  matrix products: 45.3 us -> 0 us
  starting transfers between devices: 43.6 us -> 0 us
  local copies, waits for them, and re-layouts: 46.7 us -> 4.82 us
  between operations: 22.6 us -> 0.69 us
    psum x4 -> x0, blocking collectives: 304 us -> none  [the longest x2 156 us: on_device(): lax.psum((data_local, object_local), ('src', 'space'))]
    pallas_call x0 -> x1, Pallas kernels: none -> 168 us  [on_device(): pl.pallas_call(functools.partial(kernel, cfg), out_shape=(jax.ShapeDtypeS...]
    all_to_all x4 -> x0, blocking collectives: 98.1 us -> none  [transform(): lax.all_to_all(depth_done, 'space', split_axis=2, concat_axis=3, tiled=True)]
    psum x2 -> x0, waiting for transfers between devices: 84.6 us -> none  [on_device(): numerator_all, power_all = lax.psum((numerator, power_sum), 'src')]
    all_to_all x6 -> x0, waiting for transfers between devices: 78.7 us -> none  [the longest x5 65.6 us: transform(): lax.all_to_all(returned, 'space', split_axis=3, concat_axis=2, tiled=True)]
    dot_general x30 -> x0, matrix products: 45.3 us -> none  [apply_table(): return jnp.einsum(pattern, table, fields, precision=lax.Precision.HIGHEST)]
    all_to_all x6 -> x0, starting transfers between devices: 43.5 us -> none  [the longest x5 29.7 us: transform(): lax.all_to_all(returned, 'space', split_axis=3, concat_axis=2, tiled=True)]
    mul x14 -> x0, other arithmetic: 16.8 us -> none  [the longest x2 11.7 us: on_device(): -object_weight * (chi_real * resid_real + chi_imag * resid_imag)]
  transfers between devices with their start and end apart: 8 -> 0, of which waited for: 7 -> 0; matrix products, arithmetic and copies ran while one was open for 2% -> 0% of each run, Pallas kernels for 0% -> 0%
where the time goes in v1:
time: 174 us
  Pallas kernels  168 us (97%)
  local copies, waits for them, and re-layouts  4.82 us (3%)
    pallas_call x1, Pallas kernels, on_device(): pl.pallas_call(functools.partial(kernel, cfg), out_shape=(jax.ShapeDtypeS...  168 us

profile of v1, /device:TPU:1, one launch (start us, length us, event | category | flops | bytes accessed | tf_op | source)
XLA Modules:
  0.0 174.0 jit_solution(7075763701954504774)
XLA Ops:
  0.6 0.7 copy.17
  1.3 0.0 copy-start
  1.3 0.0 copy-start.1
  1.3 0.0 copy-start.2
  1.4 1.2 copy.8
  2.6 0.0 copy-start.3
  2.6 0.0 copy-done
  2.6 0.0 copy-done.1
  2.6 0.0 copy-done.2
  2.6 0.6 copy-done.3
  3.2 168.4 %shard_map.77 = (f32[4,128,256]{2,1,0:T(8,128)S(1)}, f32[4,128,256]{2,1,0:T(8,128)S(1)}) custom-call(s32[1,2]{1,0:T(1,128)S(1)} %copy-done.3, f32[4,128,256]{2,1,0:T(8,128)S(1)} %bitcast.17, f32[4,2,256]{2,1,0:T(2,128)S(1)} %bitcast.20, f32[4,64,256]{2,1,0:T(8,128)S(1)} %copy-done.2, bf16[2,256,256]{2,1,0:T(8,128)(2,1)S(1)} %copy-done.1, ...), custom_call_target="tpu_custom_call" | custom-call | tf_op jit(solution)/shard_map/pallas_call | solution.py:484
  171.7 1.1 copy.16
  172.8 1.1 copy.15
Async XLA Ops:
  1.3 1.3 copy-start
  1.3 1.3 copy-start.1
  1.3 1.3 copy-start.2
  2.6 0.7 copy-start.3

commit v2 on v1

--- a/solution.py
+++ b/solution.py
@@ -77,8 +77,8 @@
     cfg,
     pos_ref, chi0_ref, meas_ref, tab_ref, hy_ref, hz_ref,
     w_ref, chi_out_ref,
-    chi1_ref, e_ref, s_ref, r_ref, d_ref, v_ref, sp_ref, np_ref, np_recv,
-    send1, send3, recv1, recv2, recv3, red1, red2,
+    chi1_ref, e_ref, s_ref, r_ref, d_ref, v_ref, b_ref, sp_all, np_ref, np_recv,
+    send1_all, send3_all, recv1, recv2, recv3, red1, red2,
     ex_send, ex_recv, red_send, red_recv, x_send, x_recv,
 ):
     ns, g1, g2, nz, ny, rows = cfg
@@ -186,13 +186,15 @@
         y = pl.multiple_of(lax.rem(part, halves) * 128, 128)
         return tuple(tab_ref[2 * which + c, pl.ds(z, 8), pl.ds(y, 128)] for c in range(2))
 
-    def spectral(lead, part):
+    def spectral(sp_ref, lead, part):
         return (tile(sp_ref, lead, part, 0)[...], tile(sp_ref, lead, part, 1)[...])
 
     def sweep_out(t):
+        sp_ref, send1 = sp_all.at[t % 2], send1_all.at[t % 2]
+
         def summarise(part):
             root = ctable(part, 0)
-            rowv = [spectral(i, part) for i in range(rows)]
+            rowv = [spectral(sp_ref, i, part) for i in range(rows)]
             ahead = rowv[0]
             for i in range(1, rows):
                 ahead = cmadd(ahead, root, rowv[i])
@@ -248,6 +250,7 @@
         take(recv1.at[t, pl.ds(1, g1 - 1)], ex_send.at[t, 0])
 
     def middle_back(t):
+        send3 = send3_all.at[t % 2]
         block_root = power(own_root(), int(math.log2(rows)))
         group_root = power(block_root, int(math.log2(g1)))
         turn = power(group_root, int(math.log2(g2)))
@@ -288,13 +291,14 @@
         take(recv2.at[t, pl.ds(1, g2 - 1)], ex_send.at[t, 1])
 
     def sweep_back(t):
+        sp_ref = sp_all.at[t % 2]
         take(recv3.at[t, pl.ds(1, g1 - 1)], ex_recv.at[t, 2])
 
         def step(k, carry):
             part = lax.rem(m - k + g1, g1)
             root = ctable(part, 0)
             kappa = ctable(part, 1)
-            rowv = [spectral(i, part) for i in range(rows)]
+            rowv = [spectral(sp_ref, i, part) for i in range(rows)]
             state = (recv3[t, k, 0], recv3[t, k, 1])
             ahead = []
             for i in range(rows):
@@ -312,18 +316,6 @@
         lax.fori_loop(0, g1, step, 0)
         take(recv3.at[t, pl.ds(1, g1 - 1)], ex_send.at[t, 2])
 
-    def convolve(t, src_ref, dst_ref, between=()):
-        hooks = list(between) + [lambda: None] * 3
-        local(src_ref, sp_ref)
-        hooks[0]()
-        sweep_out(t)
-        middle_out(t)
-        hooks[1]()
-        middle_back(t)
-        sweep_back(t)
-        hooks[2]()
-        local(sp_ref, dst_ref)
-
     def pair(ref, x, z):
         return (ref[x, pl.ds(z, 8), :], ref[x, pl.ds(nz + z, 8), :])
 
@@ -335,7 +327,7 @@
         def outer(n, carry):
             return body(n // zgroups, pl.multiple_of(lax.rem(n, zgroups) * 8, 8), carry)
 
-        return lax.fori_loop(0, rows * zgroups, outer, init, unroll=2)
+        return lax.fori_loop(0, rows * zgroups, outer, init, unroll=4)
 
     def square(value):
         return value[0] * value[0] + value[1] * value[1]
@@ -368,12 +360,19 @@
     for h in range(1, halves):
         data_fold = data_fold + data_part[:, h * 128:(h + 1) * 128]
 
+    local(w_ref, sp_all.at[0])
     pl.semaphore_wait(barrier, (g1 - 1) + (ns * g2 - 1))
+    sweep_out(0)
     reduce_start(0, [data_fold, fold(object_part)])
-    convolve(0, w_ref, s_ref, (lambda: reduce_middle(0),))
+    middle_out(0)
+    reduce_middle(0)
+    middle_back(0)
     sums = reduce_end(0)
+    sweep_back(0)
+    local(sp_all.at[0], s_ref)
     data_weight = 1.0 / sums[0:1]
     object_weight = 1.0 / sums[1:2]
+    ratio = 0.5 / DAMPING
     chi_ref = chi0_ref
     for update in range(OUTER):
         t = 1 + 2 * update
@@ -387,29 +386,41 @@
             put(r_ref, x, z, res)
             flipped = cmul(chi, (res[0], -res[1]))
             put(v_ref, x, z, (-flipped[0], -flipped[1]))
+            put(b_ref, x, z, (res[0] + ratio * flipped[1], res[1] + ratio * flipped[0]))
             return carry
 
         each_block(residual, 0)
         for x in range(rows):
-            v_ref[x, pl.ds(0, 1), :] += data_weight * (meas_ref[x, pl.ds(0, 1), :] - s_ref[x, pl.ds(0, 1), :])
-            v_ref[x, pl.ds(nz, 1), :] -= data_weight * (meas_ref[x, pl.ds(1, 1), :] - s_ref[x, pl.ds(nz, 1), :])
-        convolve(t, v_ref, d_ref)
-
-        def descend(x, z, total):
-            res, image = pair(r_ref, x, z), pair(d_ref, x, z)
+            top = data_weight * (meas_ref[x, pl.ds(0, 1), :] - s_ref[x, pl.ds(0, 1), :])
+            bottom = data_weight * (meas_ref[x, pl.ds(1, 1), :] - s_ref[x, pl.ds(nz, 1), :])
+            v_ref[x, pl.ds(0, 1), :] += top
+            v_ref[x, pl.ds(nz, 1), :] -= bottom
+            b_ref[x, pl.ds(0, 1), :] += ratio * bottom
+            b_ref[x, pl.ds(nz, 1), :] -= ratio * top
+        first, second = sp_all.at[t % 2], sp_all.at[(t + 1) % 2]
+        local(v_ref, first)
+        sweep_out(t)
+        local(b_ref, second)
+        sweep_out(t + 1)
+        middle_out(t)
+        middle_out(t + 1)
+        middle_back(t)
+        middle_back(t + 1)
+        sweep_back(t)
+        local(first, d_ref)
+        sweep_back(t + 1)
+        local(second, v_ref)
+
+        def descend(x, z, totals, chi_ref=chi_ref):
+            res, image, other = pair(r_ref, x, z), pair(d_ref, x, z), pair(v_ref, x, z)
             d = (res[0] + image[0], res[1] - image[1])
+            h = (other[0] + ratio * image[1], other[1] + ratio * image[0])
             put(d_ref, x, z, d)
-            return total + square(d)
-
-        descent_part = each_block(descend, zero)
-        convolve(t + 1, d_ref, v_ref)
-
-        def changes(x, z, total, chi_ref=chi_ref):
-            chi, d, h = pair(chi_ref, x, z), pair(d_ref, x, z), pair(v_ref, x, z)
-            moved = cmul(chi, h)
-            return total + square((d[0] - moved[0], d[1] - moved[1]))
-
-        change_part = each_block(changes, zero)
+            put(v_ref, x, z, h)
+            moved = cmul(pair(chi_ref, x, z), h)
+            return totals[0] + square(d), totals[1] + square((d[0] - moved[0], d[1] - moved[1]))
+
+        descent_part, change_part = each_block(descend, (zero, zero))
         image_part = jnp.zeros((1, ny), F32)
         for x in range(rows):
             image_part = image_part + square((v_ref[x, pl.ds(0, 1), :], v_ref[x, pl.ds(nz, 1), :]))
@@ -487,10 +498,11 @@
         in_specs=[pl.BlockSpec(memory_space=pltpu.SMEM)] + [vmem] * 5,
         out_specs=(vmem, vmem),
         scratch_shapes=[pltpu.VMEM(field, F32)] * 7 + [
+            pltpu.VMEM((2,) + field, F32),
             pltpu.VMEM((rows, 3 * nz, ny), F32),
             pltpu.VMEM((OUTER, ns, 3 * nz, ny), F32),
-            pltpu.VMEM((g1, 4, 8, 128), F32),
-            pltpu.VMEM((g1, 4, 8, 128), F32),
+            pltpu.VMEM((2, g1, 4, 8, 128), F32),
+            pltpu.VMEM((2, g1, 4, 8, 128), F32),
             pltpu.VMEM((transforms, g1, 4, 8, 128), F32),
             pltpu.VMEM((transforms, g2, 4, 8, 128), F32),
             pltpu.VMEM((transforms, g1, 4, 8, 128), F32),

time: 174 us -> 143 us (0.82)
  Pallas kernels: 168 us -> 137 us
    pallas_call x1, Pallas kernels: 168 us -> 137 us  [on_device(): pl.pallas_call(functools.partial(kernel, cfg), out_shape=(jax.ShapeDtypeS...]
where the time goes in v2:
time: 143 us; the launch traced here: 142 us
  Pallas kernels  137 us (96%)
  local copies, waits for them, and re-layouts  4.82 us (3%)
    pallas_call x1, Pallas kernels, on_device(): pl.pallas_call(functools.partial(kernel, cfg), out_shape=(jax.ShapeDtypeS...  137 us

profile of v2, /device:TPU:1, one launch (start us, length us, event | category | flops | bytes accessed | tf_op | source)
XLA Modules:
  0.0 142.4 jit_solution(552364022883587692)
XLA Ops:
  0.6 0.7 copy.17
  1.3 0.0 copy-start
  1.3 0.0 copy-start.1
  1.3 0.0 copy-start.2
  1.4 1.2 copy.8
  2.6 0.0 copy-start.3
  2.6 0.0 copy-done
  2.6 0.0 copy-done.1
  2.6 0.0 copy-done.2
  2.6 0.6 copy-done.3
  3.2 136.9 %shard_map.77 = (f32[4,128,256]{2,1,0:T(8,128)S(1)}, f32[4,128,256]{2,1,0:T(8,128)S(1)}) custom-call(s32[1,2]{1,0:T(1,128)S(1)} %copy-done.3, f32[4,128,256]{2,1,0:T(8,128)S(1)} %bitcast.17, f32[4,2,256]{2,1,0:T(2,128)S(1)} %bitcast.20, f32[4,64,256]{2,1,0:T(8,128)S(1)} %copy-done.2, bf16[2,256,256]{2,1,0:T(8,128)(2,1)S(1)} %copy-done.1, ...), custom_call_target="tpu_custom_call" | custom-call | tf_op jit(solution)/shard_map/pallas_call | solution.py:495
  140.1 1.1 copy.16
  141.3 1.1 copy.15
Async XLA Ops:
  1.3 1.3 copy-start
  1.3 1.3 copy-start.1
  1.3 1.3 copy-start.2
  2.6 0.7 copy-start.3

commit v3 on v2

--- a/solution.py
+++ b/solution.py
@@ -77,7 +77,7 @@
     cfg,
     pos_ref, chi0_ref, meas_ref, tab_ref, hy_ref, hz_ref,
     w_ref, chi_out_ref,
-    chi1_ref, e_ref, s_ref, r_ref, d_ref, v_ref, b_ref, sp_all, np_ref, np_recv,
+    chi1_ref, e_ref, s_ref, r_ref, d_ref, v_ref, b_ref, sp_all, rho_ref, early_ref, early_recv, late_ref, late_recv,
     send1_all, send3_all, recv1, recv2, recv3, red1, red2,
     ex_send, ex_recv, red_send, red_recv, x_send, x_recv,
 ):
@@ -189,12 +189,17 @@
     def spectral(sp_ref, lead, part):
         return (tile(sp_ref, lead, part, 0)[...], tile(sp_ref, lead, part, 1)[...])
 
-    def sweep_out(t):
+    def sweep_out(t, extra=None):
         sp_ref, send1 = sp_all.at[t % 2], send1_all.at[t % 2]
 
         def summarise(part):
             root = ctable(part, 0)
             rowv = [spectral(sp_ref, i, part) for i in range(rows)]
+            if extra is not None:
+                rowv = [extra(i, part, value) for i, value in enumerate(rowv)]
+                for i in range(rows):
+                    tile(sp_ref, i, part, 0)[...] = rowv[i][0]
+                    tile(sp_ref, i, part, 1)[...] = rowv[i][1]
             ahead = rowv[0]
             for i in range(1, rows):
                 ahead = cmadd(ahead, root, rowv[i])
@@ -370,38 +375,67 @@
     sums = reduce_end(0)
     sweep_back(0)
     local(sp_all.at[0], s_ref)
-    data_weight = 1.0 / sums[0:1]
-    object_weight = 1.0 / sums[1:2]
+    data_total = sums[0:1]
+    object_share = sums[1:2] / data_total
     ratio = 0.5 / DAMPING
+    level_zero = 1.0 / math.sqrt(nz)
     chi_ref = chi0_ref
     for update in range(OUTER):
         t = 1 + 2 * update
-        chi_next = chi1_ref if update < OUTER - 1 else chi_out_ref
-
-        def residual(x, z, carry, chi_ref=chi_ref, object_weight=object_weight):
-            chi = pair(chi_ref, x, z)
-            e, s, w = pair(e_ref, x, z), pair(s_ref, x, z), pair(w_ref, x, z)
-            field = cmul(chi, (e[0] + s[0], e[1] + s[1]))
-            res = (object_weight * (field[0] - w[0]), object_weight * (field[1] - w[1]))
-            put(r_ref, x, z, res)
-            flipped = cmul(chi, (res[0], -res[1]))
-            put(v_ref, x, z, (-flipped[0], -flipped[1]))
-            put(b_ref, x, z, (res[0] + ratio * flipped[1], res[1] + ratio * flipped[0]))
-            return carry
-
-        each_block(residual, 0)
-        for x in range(rows):
-            top = data_weight * (meas_ref[x, pl.ds(0, 1), :] - s_ref[x, pl.ds(0, 1), :])
-            bottom = data_weight * (meas_ref[x, pl.ds(1, 1), :] - s_ref[x, pl.ds(nz, 1), :])
-            v_ref[x, pl.ds(0, 1), :] += top
-            v_ref[x, pl.ds(nz, 1), :] -= bottom
-            b_ref[x, pl.ds(0, 1), :] += ratio * bottom
-            b_ref[x, pl.ds(nz, 1), :] -= ratio * top
+        a = 1 + 2 * update
+        last = update == OUTER - 1
+        chi_next = chi_out_ref if last else chi1_ref
+        early, late = early_recv.at[update], late_recv.at[update]
+
+        for k in (2, 1, 3, 0):
+            x = lax.rem(src + k, ns)
+
+            def residual(n, carry, x=x, chi_ref=chi_ref):
+                z = pl.multiple_of(n * 8, 8)
+                chi = pair(chi_ref, x, z)
+                e, s, w = pair(e_ref, x, z), pair(s_ref, x, z), pair(w_ref, x, z)
+                u = (e[0] + s[0], e[1] + s[1])
+                field = cmul(chi, u)
+                res = (field[0] - w[0], field[1] - w[1])
+                put(r_ref, x, z, res)
+                flipped = cmul(chi, (res[0], -res[1]))
+                put(v_ref, x, z, (-flipped[0], -flipped[1]))
+                put(b_ref, x, z, (res[0] + ratio * flipped[1], res[1] + ratio * flipped[0]))
+                early_ref[x, pl.ds(z, 8), :] = w[0] * u[0] + w[1] * u[1]
+                early_ref[x, pl.ds(nz + z, 8), :] = w[1] * u[0] - w[0] * u[1]
+                early_ref[x, pl.ds(2 * nz + z, 8), :] = square(u)
+                return carry
+
+            lax.fori_loop(0, zgroups, residual, 0, unroll=4)
+            if k:
+                remote(early_ref.at[x], early.at[k], x_send.at[update, 0], x_recv.at[update, 0], (x, space)).start()
+        rho = jnp.concatenate(
+            [
+                meas_ref[x, pl.ds(c, 1), :] - s_ref[x, pl.ds(c * nz, 1), :]
+                for x in range(rows) for c in range(2)
+            ],
+            axis=0,
+        )
+        rho_ref[...] = level_zero * dot3(split(rho), (hy_ref[0], hy_ref[1]))
+
         first, second = sp_all.at[t % 2], sp_all.at[(t + 1) % 2]
         local(v_ref, first)
-        sweep_out(t)
         local(b_ref, second)
-        sweep_out(t + 1)
+        if update:
+            object_share = float(ns) * reduce_end(2)[0:1] / data_total
+
+        def rho_tile(i, part, c, object_share=object_share):
+            y = pl.multiple_of(lax.rem(part, halves) * 128, 128)
+            return object_share * rho_ref[pl.ds(2 * i + c, 1), pl.ds(y, 128)]
+
+        def add_first(i, part, value, rho_tile=rho_tile):
+            return value[0] + rho_tile(i, part, 0), value[1] - rho_tile(i, part, 1)
+
+        def add_second(i, part, value, rho_tile=rho_tile):
+            return value[0] + ratio * rho_tile(i, part, 1), value[1] - ratio * rho_tile(i, part, 0)
+
+        sweep_out(t, add_first)
+        sweep_out(t + 1, add_second)
         middle_out(t)
         middle_out(t + 1)
         middle_back(t)
@@ -411,72 +445,90 @@
         sweep_back(t + 1)
         local(second, v_ref)
 
-        def descend(x, z, totals, chi_ref=chi_ref):
-            res, image, other = pair(r_ref, x, z), pair(d_ref, x, z), pair(v_ref, x, z)
-            d = (res[0] + image[0], res[1] - image[1])
-            h = (other[0] + ratio * image[1], other[1] + ratio * image[0])
-            put(d_ref, x, z, d)
-            put(v_ref, x, z, h)
-            moved = cmul(pair(chi_ref, x, z), h)
-            return totals[0] + square(d), totals[1] + square((d[0] - moved[0], d[1] - moved[1]))
-
-        descent_part, change_part = each_block(descend, (zero, zero))
+        totals = (zero, zero)
+        for k in (2, 1, 3, 0):
+            x = lax.rem(src + k, ns)
+
+            def descend(n, totals, x=x, chi_ref=chi_ref):
+                z = pl.multiple_of(n * 8, 8)
+                res, image, other = pair(r_ref, x, z), pair(d_ref, x, z), pair(v_ref, x, z)
+                d = (res[0] + image[0], res[1] - image[1])
+                h = (other[0] + ratio * image[1], other[1] + ratio * image[0])
+                put(d_ref, x, z, d)
+                put(v_ref, x, z, h)
+                moved = cmul(pair(chi_ref, x, z), h)
+                e, s, w = pair(e_ref, x, z), pair(s_ref, x, z), pair(w_ref, x, z)
+                u = (e[0] + s[0], e[1] + s[1])
+                late_parts = (
+                    d[0] * u[0] + d[1] * u[1] + (w[0] * h[0] + w[1] * h[1]),
+                    d[1] * u[0] - d[0] * u[1] + (w[1] * h[0] - w[0] * h[1]),
+                    2.0 * (u[0] * h[0] + u[1] * h[1]),
+                    d[0] * h[0] + d[1] * h[1],
+                    d[1] * h[0] - d[0] * h[1],
+                    square(h),
+                )
+                for c, value in enumerate(late_parts):
+                    late_ref[x, pl.ds(c * nz + z, 8), :] = value
+                return totals[0] + square(d), totals[1] + square((d[0] - moved[0], d[1] - moved[1]))
+
+            totals = lax.fori_loop(0, zgroups, descend, totals, unroll=4)
+            if k:
+                remote(late_ref.at[x], late.at[k], x_send.at[update, 1], x_recv.at[update, 1], (x, space)).start()
         image_part = jnp.zeros((1, ny), F32)
         for x in range(rows):
             image_part = image_part + square((v_ref[x, pl.ds(0, 1), :], v_ref[x, pl.ds(nz, 1), :]))
         image_fold = image_part[:, :128]
         for h in range(1, halves):
             image_fold = image_fold + image_part[:, h * 128:(h + 1) * 128]
-        a = 1 + 2 * update
-        reduce_start(a, [fold(descent_part), image_fold, fold(change_part)])
+        reduce_start(a, [fold(totals[0]), image_fold, fold(totals[1])])
+        take(early.at[pl.ds(1, ns - 1)], x_recv.at[update, 0])
+
+        def gather_early(n, carry, early=early):
+            at = pl.ds(pl.multiple_of(n * 8, 8), 8)
+            early_ref[src, at, :] = early_ref[src, at, :] + early[1, at, :] + early[2, at, :] + early[3, at, :]
+            return carry
+
+        lax.fori_loop(0, 3 * zgroups, gather_early, 0, unroll=4)
         reduce_middle(a)
         sums = reduce_end(a)
-        length = sums[0:1] / (data_weight * sums[1:2] + object_weight * sums[2:3])
-
-        for k in range(1, ns + 1):
-            x = lax.rem(src + k, ns)
-
-            def advance(n, carry, x=x, length=length):
-                z = pl.multiple_of(n * 8, 8)
-                w, s, d, h, e = (pair(ref, x, z) for ref in (w_ref, s_ref, d_ref, v_ref, e_ref))
-                w = (w[0] + length * d[0], w[1] + length * d[1])
-                s = (s[0] + length * h[0], s[1] + length * h[1])
-                put(w_ref, x, z, w)
-                put(s_ref, x, z, s)
-                u = (e[0] + s[0], e[1] + s[1])
-                np_ref[x, pl.ds(z, 8), :] = w[0] * u[0] + w[1] * u[1]
-                np_ref[x, pl.ds(nz + z, 8), :] = w[1] * u[0] - w[0] * u[1]
-                np_ref[x, pl.ds(2 * nz + z, 8), :] = square(u)
-                return carry
-
-            lax.fori_loop(0, zgroups, advance, 0, unroll=2)
-            if k < ns:
-                remote(np_ref.at[x], np_recv.at[update, k], x_send.at[update, 0], x_recv.at[update, 0],
-                       (x, space)).start()
-        take(np_recv.at[update, pl.ds(1, ns - 1)], x_recv.at[update, 0])
-
-        def contrast(n, total):
+        length = sums[0:1] / (object_share * sums[1:2] + sums[2:3])
+
+        def advance(x, z, carry, length=length, last=last):
+            w, d = pair(w_ref, x, z), pair(d_ref, x, z)
+            put(w_ref, x, z, (w[0] + length * d[0], w[1] + length * d[1]))
+            if not last:
+                s, h = pair(s_ref, x, z), pair(v_ref, x, z)
+                put(s_ref, x, z, (s[0] + length * h[0], s[1] + length * h[1]))
+            return carry
+
+        each_block(advance, 0)
+        take(late.at[pl.ds(1, ns - 1)], x_recv.at[update, 1])
+
+        def contrast(n, total, length=length, late=late, chi_next=chi_next):
             z = pl.multiple_of(n * 8, 8)
-            parts = [np_ref[src, pl.ds(c * nz + z, 8), :] for c in range(3)]
-            for k in range(1, ns):
-                parts = [parts[c] + np_recv[update, k, pl.ds(c * nz + z, 8), :] for c in range(3)]
+            sums = []
+            for c in range(6):
+                at = pl.ds(c * nz + z, 8)
+                sums.append(late_ref[src, at, :] + late[1, at, :] + late[2, at, :] + late[3, at, :])
+            parts = [
+                early_ref[src, pl.ds(c * nz + z, 8), :] + length * (sums[c] + length * sums[3 + c]) for c in range(3)
+            ]
             scale = 1.0 / jnp.maximum(parts[2], FLOOR_SHARE * ns)
             chi = (jnp.clip(parts[0] * scale, REAL_LOW, REAL_HIGH), jnp.clip(parts[1] * scale, 0.0, IMAG_HIGH))
             put(chi_next, src, z, chi)
             return total + square(chi)
 
         chi_part = lax.fori_loop(0, zgroups, contrast, zero, unroll=2)
-        for k in range(1, ns):
-            remote(chi_next.at[src], chi_next.at[src], x_send.at[update, 1], x_recv.at[update, 1],
+        for k in (2, 1, 3):
+            remote(chi_next.at[src], chi_next.at[src], x_send.at[update, 2], x_recv.at[update, 2],
                    (lax.rem(src + k, ns), space)).start()
-        if update < OUTER - 1:
-            reduce_start(a + 1, [fold(chi_part) * float(ns)])
-            reduce_middle(a + 1)
-            sums = reduce_end(a + 1)
-            object_weight = 1.0 / sums[0:1]
-        take(chi_next.at[pl.ds(0, ns - 1)], x_recv.at[update, 1])
-        take(np_recv.at[update, pl.ds(1, ns - 1)], x_send.at[update, 0])
-        take(chi_next.at[pl.ds(0, ns - 1)], x_send.at[update, 1])
+        if not last:
+            reduce_start(2, [fold(chi_part)])
+            reduce_middle(2)
+        take(chi_next.at[pl.ds(0, ns - 1)], x_recv.at[update, 2])
+        take(early.at[pl.ds(1, ns - 1)], x_send.at[update, 0])
+        take(late.at[pl.ds(1, ns - 1)], x_send.at[update, 1])
+        take(chi_next.at[pl.ds(0, ns - 1)], x_send.at[update, 2])
         chi_ref = chi_next
 
 
@@ -499,8 +551,11 @@
         out_specs=(vmem, vmem),
         scratch_shapes=[pltpu.VMEM(field, F32)] * 7 + [
             pltpu.VMEM((2,) + field, F32),
+            pltpu.VMEM((2 * rows, ny), F32),
             pltpu.VMEM((rows, 3 * nz, ny), F32),
             pltpu.VMEM((OUTER, ns, 3 * nz, ny), F32),
+            pltpu.VMEM((rows, 6 * nz, ny), F32),
+            pltpu.VMEM((OUTER, ns, 6 * nz, ny), F32),
             pltpu.VMEM((2, g1, 4, 8, 128), F32),
             pltpu.VMEM((2, g1, 4, 8, 128), F32),
             pltpu.VMEM((transforms, g1, 4, 8, 128), F32),
@@ -512,8 +567,8 @@
             pltpu.SemaphoreType.DMA((transforms, 3)),
             pltpu.SemaphoreType.DMA((reductions, 2)),
             pltpu.SemaphoreType.DMA((reductions, 2)),
-            pltpu.SemaphoreType.DMA((OUTER, 2)),
-            pltpu.SemaphoreType.DMA((OUTER, 2)),
+            pltpu.SemaphoreType.DMA((OUTER, 3)),
+            pltpu.SemaphoreType.DMA((OUTER, 3)),
         ],
         compiler_params=pltpu.CompilerParams(
             collective_id=0, has_side_effects=True, vmem_limit_bytes=40 * 1024 * 1024

time: 143 us -> 141 us (0.986)
  no operation moved by 1% of the time
where the time goes in v3:
time: 141 us
  Pallas kernels  136 us (96%)
  local copies, waits for them, and re-layouts  4.82 us (3%)
    pallas_call x1, Pallas kernels, on_device(): pl.pallas_call(functools.partial(kernel, cfg), out_shape=(jax.ShapeDtypeS...  136 us

profile of v3, /device:TPU:1, one launch (start us, length us, event | category | flops | bytes accessed | tf_op | source)
XLA Modules:
  0.0 141.0 jit_solution(6599934078785465486)
XLA Ops:
  0.6 0.7 copy.17
  1.3 0.0 copy-start
  1.3 0.0 copy-start.1
  1.3 0.0 copy-start.2
  1.4 1.2 copy.8
  2.6 0.0 copy-start.3
  2.6 0.0 copy-done
  2.6 0.0 copy-done.1
  2.6 0.0 copy-done.2
  2.6 0.6 copy-done.3
  3.2 135.5 %shard_map.77 = (f32[4,128,256]{2,1,0:T(8,128)S(1)}, f32[4,128,256]{2,1,0:T(8,128)S(1)}) custom-call(s32[1,2]{1,0:T(1,128)S(1)} %copy-done.3, f32[4,128,256]{2,1,0:T(8,128)S(1)} %bitcast.17, f32[4,2,256]{2,1,0:T(2,128)S(1)} %bitcast.20, f32[4,64,256]{2,1,0:T(8,128)S(1)} %copy-done.2, bf16[2,256,256]{2,1,0:T(8,128)(2,1)S(1)} %copy-done.1, ...), custom_call_target="tpu_custom_call" | custom-call | tf_op jit(solution)/shard_map/pallas_call | solution.py:547
  138.8 1.1 copy.16
  139.9 1.1 copy.15
Async XLA Ops:
  1.3 1.3 copy-start
  1.3 1.3 copy-start.1
  1.3 1.3 copy-start.2
  2.6 0.7 copy-start.3

commit v4 on v3

--- a/solution.py
+++ b/solution.py
@@ -78,7 +78,7 @@
     pos_ref, chi0_ref, meas_ref, tab_ref, hy_ref, hz_ref,
     w_ref, chi_out_ref,
     chi1_ref, e_ref, s_ref, r_ref, d_ref, v_ref, b_ref, sp_all, rho_ref, early_ref, early_recv, late_ref, late_recv,
-    send1_all, send3_all, recv1, recv2, recv3, red1, red2,
+    send0_all, send1_all, send3_all, states_all, sums, recv1, recv2, recv3, recv4, red1, red2,
     ex_send, ex_recv, red_send, red_recv, x_send, x_recv,
 ):
     ns, g1, g2, nz, ny, rows = cfg
@@ -88,8 +88,13 @@
     src = lax.axis_index("src")
     space = lax.axis_index("space")
     m = lax.rem(space, g1)
+    chips = g1 // 2
+    core = lax.rem(m, 2)
+    chip = m // 2
     grp = space // g1
     base = grp * g1
+
+    partner = (src, space + 1 - 2 * core)
 
     barrier = pltpu.get_barrier_semaphore()
 
@@ -190,7 +195,7 @@
         return (tile(sp_ref, lead, part, 0)[...], tile(sp_ref, lead, part, 1)[...])
 
     def sweep_out(t, extra=None):
-        sp_ref, send1 = sp_all.at[t % 2], send1_all.at[t % 2]
+        sp_ref, send0, send1 = sp_all.at[t % 2], send0_all.at[t % 2], send1_all.at[t % 2]
 
         def summarise(part):
             root = ctable(part, 0)
@@ -208,16 +213,42 @@
                 behind = cmadd(behind, root, rowv[i])
             return ahead + behind
 
+        def other_half(k, carry):
+            g = lax.rem(chip + k, chips)
+            vals = summarise(2 * g + 1 - core)
+            for c in range(4):
+                send0[g, c] = vals[c]
+            remote(send0.at[g], sums.at[t, core, g], ex_send.at[t, 0], ex_recv.at[t, 0], partner).start()
+            return carry
+
+        def own_half(k, carry):
+            g = lax.rem(chip + k, chips)
+            vals = summarise(2 * g + core)
+            for c in range(4):
+                sums[t, core, g, c] = vals[c]
+            return carry
+
+        lax.fori_loop(1, chips + 1, other_half, 0, unroll=2)
+        lax.fori_loop(1, chips + 1, own_half, 0, unroll=2)
+        take(sums.at[t, 1 - core], ex_recv.at[t, 0])
+
+        def combine(g):
+            block_root = power(ctable(2 * g + core, 0), int(math.log2(rows)))
+            first = [sums[t, 0, g, c] for c in range(4)]
+            second = [sums[t, 1, g, c] for c in range(4)]
+            return cmadd(first[:2], block_root, second[:2]) + cmadd(second[2:], block_root, first[2:])
+
         def step(k, carry):
-            peer = lax.rem(m + k, g1)
-            vals = summarise(peer)
+            g = lax.rem(chip + k, chips)
+            vals = combine(g)
             for c in range(4):
-                send1[peer, c] = vals[c]
-            remote(send1.at[peer], recv1.at[t, k], ex_send.at[t, 0], ex_recv.at[t, 0], (src, base + peer)).start()
-            return carry
-
-        lax.fori_loop(1, g1, step, 0)
-        vals = summarise(m)
+                send1[g, c] = vals[c]
+            remote(send1.at[g], recv1.at[t, k], ex_send.at[t, 1], ex_recv.at[t, 1],
+                   (src, base + 2 * g + core)).start()
+            return carry
+
+        lax.fori_loop(1, chips, step, 0)
+        vals = combine(chip)
         for c in range(4):
             recv1[t, 0, c] = vals[c]
 
@@ -229,40 +260,42 @@
     def own_root():
         return ctable(m, 0)
 
+    def chip_root():
+        return power(own_root(), int(math.log2(2 * rows)))
+
     def middle_out(t):
-        take(recv1.at[t, pl.ds(1, g1 - 1)], ex_recv.at[t, 0])
-        block_root = power(own_root(), int(math.log2(rows)))
+        take(recv1.at[t, pl.ds(1, chips - 1)], ex_recv.at[t, 1])
+        root = chip_root()
 
         def gather(j, carry):
             ahead, behind = carry
-            slot_a = lax.rem(m - j + g1, g1)
-            slot_b = lax.rem(m - (g1 - 1 - j) + g1, g1)
-            ahead = cmadd(ahead, block_root, (recv1[t, slot_a, 0], recv1[t, slot_a, 1]))
-            behind = cmadd(behind, block_root, (recv1[t, slot_b, 2], recv1[t, slot_b, 3]))
+            slot_a = lax.rem(chip - j + chips, chips)
+            slot_b = lax.rem(chip + 1 + j, chips)
+            ahead = cmadd(ahead, root, (recv1[t, slot_a, 0], recv1[t, slot_a, 1]))
+            behind = cmadd(behind, root, (recv1[t, slot_b, 2], recv1[t, slot_b, 3]))
             return ahead, behind
 
         zero = jnp.zeros((8, 128), F32)
-        ahead, behind = lax.fori_loop(0, g1, gather, ((zero, zero), (zero, zero)), unroll=True)
+        ahead, behind = lax.fori_loop(0, chips, gather, ((zero, zero), (zero, zero)), unroll=True)
         for c, value in enumerate(ahead + behind):
             recv2[t, 0, c] = value
 
         def send(k, carry):
             peer = lax.rem(grp + k, g2) * g1 + m
-            remote(recv2.at[t, 0], recv2.at[t, k], ex_send.at[t, 1], ex_recv.at[t, 1], (src, peer)).start()
+            remote(recv2.at[t, 0], recv2.at[t, k], ex_send.at[t, 2], ex_recv.at[t, 2], (src, peer)).start()
             return carry
 
         lax.fori_loop(1, g2, send, 0)
-        take(recv1.at[t, pl.ds(1, g1 - 1)], ex_send.at[t, 0])
 
     def middle_back(t):
         send3 = send3_all.at[t % 2]
-        block_root = power(own_root(), int(math.log2(rows)))
-        group_root = power(block_root, int(math.log2(g1)))
+        root = chip_root()
+        group_root = power(root, int(math.log2(chips)))
         turn = power(group_root, int(math.log2(g2)))
         real, imag = 1.0 - turn[0], turn[1]
         norm = 1.0 / (real * real + imag * imag)
         inverse = (real * norm, imag * norm)
-        take(recv2.at[t, pl.ds(1, g2 - 1)], ex_recv.at[t, 1])
+        take(recv2.at[t, pl.ds(1, g2 - 1)], ex_recv.at[t, 2])
         left = (recv2[t, 0, 0], recv2[t, 0, 1])
         right = (recv2[t, 0, 2], recv2[t, 0, 3])
         for k in range(g2 - 1, 0, -1):
@@ -273,53 +306,84 @@
 
         def spread(j, carry):
             left, right = carry
-            back = g1 - 1 - j
+            back = chips - 1 - j
             for c in range(2):
                 send3[j, c] = left[c]
                 send3[back, 2 + c] = right[c]
-            slot_a = lax.rem(m - j + g1, g1)
-            slot_b = lax.rem(m - back + g1, g1)
-            left = cmadd(left, block_root, (recv1[t, slot_a, 0], recv1[t, slot_a, 1]))
-            right = cmadd(right, block_root, (recv1[t, slot_b, 2], recv1[t, slot_b, 3]))
+            slot_a = lax.rem(chip - j + chips, chips)
+            slot_b = lax.rem(chip + 1 + j, chips)
+            left = cmadd(left, root, (recv1[t, slot_a, 0], recv1[t, slot_a, 1]))
+            right = cmadd(right, root, (recv1[t, slot_b, 2], recv1[t, slot_b, 3]))
             return left, right
 
-        lax.fori_loop(0, g1, spread, (left, right), unroll=True)
+        lax.fori_loop(0, chips, spread, (left, right), unroll=True)
 
         def send(k, carry):
-            peer = lax.rem(m + k, g1)
-            remote(send3.at[peer], recv3.at[t, k], ex_send.at[t, 2], ex_recv.at[t, 2], (src, base + peer)).start()
-            return carry
-
-        lax.fori_loop(1, g1, send, 0)
+            g = lax.rem(chip + k, chips)
+            remote(send3.at[g], recv3.at[t, k], ex_send.at[t, 3], ex_recv.at[t, 3],
+                   (src, base + 2 * g + core)).start()
+            return carry
+
+        lax.fori_loop(1, chips, send, 0)
         for c in range(4):
-            recv3[t, 0, c] = send3[m, c]
-        take(recv2.at[t, pl.ds(1, g2 - 1)], ex_send.at[t, 1])
+            recv3[t, 0, c] = send3[chip, c]
 
     def sweep_back(t):
-        sp_ref = sp_all.at[t % 2]
-        take(recv3.at[t, pl.ds(1, g1 - 1)], ex_recv.at[t, 2])
-
-        def step(k, carry):
-            part = lax.rem(m - k + g1, g1)
+        sp_ref, states = sp_all.at[t % 2], states_all.at[t % 2]
+        take(recv3.at[t, pl.ds(1, chips - 1)], ex_recv.at[t, 3])
+
+        def pass_on(k, carry):
+            g = lax.rem(chip - k + chips, chips)
+            block_root = power(ctable(2 * g + core, 0), int(math.log2(rows)))
+            left = (recv3[t, k, 0], recv3[t, k, 1])
+            right = (recv3[t, k, 2], recv3[t, k, 3])
+            inner_left = cmadd(left, block_root, (sums[t, 0, g, 0], sums[t, 0, g, 1]))
+            inner_right = cmadd(right, block_root, (sums[t, 1, g, 2], sums[t, 1, g, 3]))
+            for c in range(2):
+                states[0, g, c] = left[c]
+                states[0, g, 2 + c] = inner_right[c]
+                states[1, g, c] = inner_left[c]
+                states[1, g, 2 + c] = right[c]
+            remote(states.at[1 - core, g], recv4.at[t, g], ex_send.at[t, 4], ex_recv.at[t, 4], partner).start()
+            return carry
+
+        lax.fori_loop(0, chips, pass_on, 0, unroll=2)
+
+        def apply(part, ends):
             root = ctable(part, 0)
             kappa = ctable(part, 1)
             rowv = [spectral(sp_ref, i, part) for i in range(rows)]
-            state = (recv3[t, k, 0], recv3[t, k, 1])
+            state = ends[:2]
             ahead = []
             for i in range(rows):
                 state = cmadd(state, root, rowv[i])
                 ahead.append(state)
-            state = cmul((recv3[t, k, 2], recv3[t, k, 3]), root)
+            state = cmul(ends[2:], root)
             for i in range(rows - 1, -1, -1):
                 total = cmul((ahead[i][0] + state[0], ahead[i][1] + state[1]), kappa)
                 tile(sp_ref, i, part, 0)[...] = total[0]
                 tile(sp_ref, i, part, 1)[...] = total[1]
                 if i:
                     state = cmul((state[0] + rowv[i][0], state[1] + rowv[i][1]), root)
-            return carry
-
-        lax.fori_loop(0, g1, step, 0)
-        take(recv3.at[t, pl.ds(1, g1 - 1)], ex_send.at[t, 2])
+
+        def own_half(g, carry):
+            apply(2 * g + core, tuple(states[core, g, c] for c in range(4)))
+            return carry
+
+        def other_half(g, carry):
+            apply(2 * g + 1 - core, tuple(recv4[t, g, c] for c in range(4)))
+            return carry
+
+        lax.fori_loop(0, chips, own_half, 0, unroll=2)
+        take(recv4.at[t], ex_recv.at[t, 4])
+        lax.fori_loop(0, chips, other_half, 0, unroll=2)
+
+    def finish(t):
+        take(recv4.at[t], ex_send.at[t, 0])
+        take(recv1.at[t, pl.ds(1, chips - 1)], ex_send.at[t, 1])
+        take(recv2.at[t, pl.ds(1, g2 - 1)], ex_send.at[t, 2])
+        take(recv3.at[t, pl.ds(1, chips - 1)], ex_send.at[t, 3])
+        take(recv4.at[t], ex_send.at[t, 4])
 
     def pair(ref, x, z):
         return (ref[x, pl.ds(z, 8), :], ref[x, pl.ds(nz + z, 8), :])
@@ -372,11 +436,12 @@
     middle_out(0)
     reduce_middle(0)
     middle_back(0)
-    sums = reduce_end(0)
+    totals = reduce_end(0)
     sweep_back(0)
+    finish(0)
     local(sp_all.at[0], s_ref)
-    data_total = sums[0:1]
-    object_share = sums[1:2] / data_total
+    data_total = totals[0:1]
+    object_share = totals[1:2] / data_total
     ratio = 0.5 / DAMPING
     level_zero = 1.0 / math.sqrt(nz)
     chi_ref = chi0_ref
@@ -444,6 +509,8 @@
         local(first, d_ref)
         sweep_back(t + 1)
         local(second, v_ref)
+        finish(t)
+        finish(t + 1)
 
         totals = (zero, zero)
         for k in (2, 1, 3, 0):
@@ -490,8 +557,8 @@
 
         lax.fori_loop(0, 3 * zgroups, gather_early, 0, unroll=4)
         reduce_middle(a)
-        sums = reduce_end(a)
-        length = sums[0:1] / (object_share * sums[1:2] + sums[2:3])
+        totals = reduce_end(a)
+        length = totals[0:1] / (object_share * totals[1:2] + totals[2:3])
 
         def advance(x, z, carry, length=length, last=last):
             w, d = pair(w_ref, x, z), pair(d_ref, x, z)
@@ -506,12 +573,12 @@
 
         def contrast(n, total, length=length, late=late, chi_next=chi_next):
             z = pl.multiple_of(n * 8, 8)
-            sums = []
+            terms = []
             for c in range(6):
                 at = pl.ds(c * nz + z, 8)
-                sums.append(late_ref[src, at, :] + late[1, at, :] + late[2, at, :] + late[3, at, :])
+                terms.append(late_ref[src, at, :] + late[1, at, :] + late[2, at, :] + late[3, at, :])
             parts = [
-                early_ref[src, pl.ds(c * nz + z, 8), :] + length * (sums[c] + length * sums[3 + c]) for c in range(3)
+                early_ref[src, pl.ds(c * nz + z, 8), :] + length * (terms[c] + length * terms[3 + c]) for c in range(3)
             ]
             scale = 1.0 / jnp.maximum(parts[2], FLOOR_SHARE * ns)
             chi = (jnp.clip(parts[0] * scale, REAL_LOW, REAL_HIGH), jnp.clip(parts[1] * scale, 0.0, IMAG_HIGH))
@@ -556,15 +623,19 @@
             pltpu.VMEM((OUTER, ns, 3 * nz, ny), F32),
             pltpu.VMEM((rows, 6 * nz, ny), F32),
             pltpu.VMEM((OUTER, ns, 6 * nz, ny), F32),
-            pltpu.VMEM((2, g1, 4, 8, 128), F32),
-            pltpu.VMEM((2, g1, 4, 8, 128), F32),
-            pltpu.VMEM((transforms, g1, 4, 8, 128), F32),
+            pltpu.VMEM((2, g1 // 2, 4, 8, 128), F32),
+            pltpu.VMEM((2, g1 // 2, 4, 8, 128), F32),
+            pltpu.VMEM((2, g1 // 2, 4, 8, 128), F32),
+            pltpu.VMEM((2, 2, g1 // 2, 4, 8, 128), F32),
+            pltpu.VMEM((transforms, 2, g1 // 2, 4, 8, 128), F32),
+            pltpu.VMEM((transforms, g1 // 2, 4, 8, 128), F32),
             pltpu.VMEM((transforms, g2, 4, 8, 128), F32),
-            pltpu.VMEM((transforms, g1, 4, 8, 128), F32),
+            pltpu.VMEM((transforms, g1 // 2, 4, 8, 128), F32),
+            pltpu.VMEM((transforms, g1 // 2, 4, 8, 128), F32),
             pltpu.VMEM((reductions, g1, 8, 128), F32),
             pltpu.VMEM((reductions, ns * g2, 8, 128), F32),
-            pltpu.SemaphoreType.DMA((transforms, 3)),
-            pltpu.SemaphoreType.DMA((transforms, 3)),
+            pltpu.SemaphoreType.DMA((transforms, 5)),
+            pltpu.SemaphoreType.DMA((transforms, 5)),
             pltpu.SemaphoreType.DMA((reductions, 2)),
             pltpu.SemaphoreType.DMA((reductions, 2)),
             pltpu.SemaphoreType.DMA((OUTER, 3)),

time: 141 us -> 136 us (0.965)
  Pallas kernels: 136 us -> 131 us
    pallas_call x1, Pallas kernels: 136 us -> 131 us  [on_device(): pl.pallas_call(functools.partial(kernel, cfg), out_shape=(jax.ShapeDtypeS...]
where the time goes in v4:
time: 136 us
  Pallas kernels  131 us (96%)
  local copies, waits for them, and re-layouts  4.82 us (4%)
    pallas_call x1, Pallas kernels, on_device(): pl.pallas_call(functools.partial(kernel, cfg), out_shape=(jax.ShapeDtypeS...  131 us

profile of v4, /device:TPU:1, one launch (start us, length us, event | category | flops | bytes accessed | tf_op | source)
XLA Modules:
  0.0 136.2 jit_solution(4881508775349153447)
XLA Ops:
  0.6 0.7 copy.17
  1.3 0.0 copy-start
  1.3 0.0 copy-start.1
  1.3 0.0 copy-start.2
  1.4 1.2 copy.8
  2.6 0.0 copy-start.3
  2.6 0.0 copy-done
  2.6 0.0 copy-done.1
  2.6 0.0 copy-done.2
  2.6 0.6 copy-done.3
  3.2 130.7 %shard_map.77 = (f32[4,128,256]{2,1,0:T(8,128)S(1)}, f32[4,128,256]{2,1,0:T(8,128)S(1)}) custom-call(s32[1,2]{1,0:T(1,128)S(1)} %copy-done.3, f32[4,128,256]{2,1,0:T(8,128)S(1)} %bitcast.17, f32[4,2,256]{2,1,0:T(2,128)S(1)} %bitcast.20, f32[4,64,256]{2,1,0:T(8,128)S(1)} %copy-done.2, bf16[2,256,256]{2,1,0:T(8,128)(2,1)S(1)} %copy-done.1, ...), custom_call_target="tpu_custom_call" | custom-call | tf_op jit(solution)/shard_map/pallas_call | solution.py:614
  134.0 1.1 copy.16
  135.1 1.1 copy.15
Async XLA Ops:
  1.3 1.3 copy-start
  1.3 1.3 copy-start.1
  1.3 1.3 copy-start.2
  2.6 0.7 copy-start.3

commit v5 on v4

--- a/solution.py
+++ b/solution.py
@@ -79,7 +79,7 @@
     w_ref, chi_out_ref,
     chi1_ref, e_ref, s_ref, r_ref, d_ref, v_ref, b_ref, sp_all, rho_ref, early_ref, early_recv, late_ref, late_recv,
     send0_all, send1_all, send3_all, states_all, sums, recv1, recv2, recv3, recv4, red1, red2,
-    ex_send, ex_recv, red_send, red_recv, x_send, x_recv,
+    ex_send, ex_recv, red_send, red_recv, x_send, x_recv, late_send, late_took, chi_took,
 ):
     ns, g1, g2, nz, ny, rows = cfg
     halves = ny // 128
@@ -451,9 +451,12 @@
         last = update == OUTER - 1
         chi_next = chi_out_ref if last else chi1_ref
         early, late = early_recv.at[update], late_recv.at[update]
-
-        for k in (2, 1, 3, 0):
+        right, left, across = (lax.rem(src + k, ns) for k in (1, 3, 2))
+
+        for k in (0, 3, 1, 2):
             x = lax.rem(src + k, ns)
+            if update and k:
+                take(chi_ref.at[0], chi_took.at[update - 1, ns - k])
 
             def residual(n, carry, x=x, chi_ref=chi_ref):
                 z = pl.multiple_of(n * 8, 8)
@@ -511,6 +514,20 @@
         local(second, v_ref)
         finish(t)
         finish(t + 1)
+
+        def pass_late(row, half, place, device, update=update, late=late):
+            remote(late_ref.at[row, half], late.at[place, half], late_send.at[update, place, half],
+                   late_took.at[update, place, half], (device, space)).start()
+
+        def add_late(row, half, update=update, late=late):
+            take(late.at[0, half], late_took.at[update, 0, half])
+
+            def add(n, carry):
+                at = pl.ds(pl.multiple_of(n * 8, 8), 8)
+                late_ref[row, half, at, :] = late_ref[row, half, at, :] + late[0, half, at, :]
+                return carry
+
+            lax.fori_loop(0, 3 * zgroups, add, 0, unroll=8)
 
         totals = (zero, zero)
         for k in (2, 1, 3, 0):
@@ -534,13 +551,19 @@
                     d[1] * h[0] - d[0] * h[1],
                     square(h),
                 )
+                half = n // (zgroups // 2)
                 for c, value in enumerate(late_parts):
-                    late_ref[x, pl.ds(c * nz + z, 8), :] = value
+                    late_ref[x, half, pl.ds(c * (nz // 2) + z - half * (nz // 2), 8), :] = value
                 return totals[0] + square(d), totals[1] + square((d[0] - moved[0], d[1] - moved[1]))
 
             totals = lax.fori_loop(0, zgroups, descend, totals, unroll=4)
-            if k:
-                remote(late_ref.at[x], late.at[k], x_send.at[update, 1], x_recv.at[update, 1], (x, space)).start()
+            if k == 2:
+                pass_late(across, 0, 0, right)
+                pass_late(across, 1, 0, left)
+            elif k == 1:
+                pass_late(right, 1, 1, right)
+            elif k == 3:
+                pass_late(left, 0, 2, left)
         image_part = jnp.zeros((1, ny), F32)
         for x in range(rows):
             image_part = image_part + square((v_ref[x, pl.ds(0, 1), :], v_ref[x, pl.ds(nz, 1), :]))
@@ -557,6 +580,10 @@
 
         lax.fori_loop(0, 3 * zgroups, gather_early, 0, unroll=4)
         reduce_middle(a)
+        add_late(right, 0)
+        pass_late(right, 0, 1, right)
+        add_late(left, 1)
+        pass_late(left, 1, 2, left)
         totals = reduce_end(a)
         length = totals[0:1] / (object_share * totals[1:2] + totals[2:3])
 
@@ -569,14 +596,17 @@
             return carry
 
         each_block(advance, 0)
-        take(late.at[pl.ds(1, ns - 1)], x_recv.at[update, 1])
+        for half in range(2):
+            for place in (1, 2):
+                take(late.at[place, half], late_took.at[update, place, half])
 
         def contrast(n, total, length=length, late=late, chi_next=chi_next):
             z = pl.multiple_of(n * 8, 8)
             terms = []
+            half = n // (zgroups // 2)
             for c in range(6):
-                at = pl.ds(c * nz + z, 8)
-                terms.append(late_ref[src, at, :] + late[1, at, :] + late[2, at, :] + late[3, at, :])
+                at = pl.ds(c * (nz // 2) + z - half * (nz // 2), 8)
+                terms.append(late_ref[src, half, at, :] + late[1, half, at, :] + late[2, half, at, :])
             parts = [
                 early_ref[src, pl.ds(c * nz + z, 8), :] + length * (terms[c] + length * terms[3 + c]) for c in range(3)
             ]
@@ -587,16 +617,21 @@
 
         chi_part = lax.fori_loop(0, zgroups, contrast, zero, unroll=2)
         for k in (2, 1, 3):
-            remote(chi_next.at[src], chi_next.at[src], x_send.at[update, 2], x_recv.at[update, 2],
+            remote(chi_next.at[src], chi_next.at[src], x_send.at[update, 1], chi_took.at[update, k],
                    (lax.rem(src + k, ns), space)).start()
         if not last:
             reduce_start(2, [fold(chi_part)])
             reduce_middle(2)
-        take(chi_next.at[pl.ds(0, ns - 1)], x_recv.at[update, 2])
+        else:
+            for k in range(1, ns):
+                take(chi_next.at[0], chi_took.at[update, k])
         take(early.at[pl.ds(1, ns - 1)], x_send.at[update, 0])
-        take(late.at[pl.ds(1, ns - 1)], x_send.at[update, 1])
-        take(chi_next.at[pl.ds(0, ns - 1)], x_send.at[update, 2])
+        for half in range(2):
+            for place in range(3):
+                take(late.at[place, half], late_send.at[update, place, half])
         chi_ref = chi_next
+    for update in range(OUTER):
+        take(chi_out_ref.at[pl.ds(0, ns - 1)], x_send.at[update, 1])
 
 
 def on_device(ns, g1, g2, contrast, measured, positions):
@@ -621,8 +656,8 @@
             pltpu.VMEM((2 * rows, ny), F32),
             pltpu.VMEM((rows, 3 * nz, ny), F32),
             pltpu.VMEM((OUTER, ns, 3 * nz, ny), F32),
-            pltpu.VMEM((rows, 6 * nz, ny), F32),
-            pltpu.VMEM((OUTER, ns, 6 * nz, ny), F32),
+            pltpu.VMEM((rows, 2, 3 * nz, ny), F32),
+            pltpu.VMEM((OUTER, 3, 2, 3 * nz, ny), F32),
             pltpu.VMEM((2, g1 // 2, 4, 8, 128), F32),
             pltpu.VMEM((2, g1 // 2, 4, 8, 128), F32),
             pltpu.VMEM((2, g1 // 2, 4, 8, 128), F32),
@@ -638,8 +673,11 @@
             pltpu.SemaphoreType.DMA((transforms, 5)),
             pltpu.SemaphoreType.DMA((reductions, 2)),
             pltpu.SemaphoreType.DMA((reductions, 2)),
-            pltpu.SemaphoreType.DMA((OUTER, 3)),
-            pltpu.SemaphoreType.DMA((OUTER, 3)),
+            pltpu.SemaphoreType.DMA((OUTER, 2)),
+            pltpu.SemaphoreType.DMA((OUTER, 2)),
+            pltpu.SemaphoreType.DMA((OUTER, 3, 2)),
+            pltpu.SemaphoreType.DMA((OUTER, 3, 2)),
+            pltpu.SemaphoreType.DMA((OUTER, ns)),
         ],
         compiler_params=pltpu.CompilerParams(
             collective_id=0, has_side_effects=True, vmem_limit_bytes=40 * 1024 * 1024

time: 136 us -> 126 us (0.926)
  Pallas kernels: 131 us -> 121 us
    pallas_call x1, Pallas kernels: 131 us -> 121 us  [on_device(): pl.pallas_call(functools.partial(kernel, cfg), out_shape=(jax.ShapeDtypeS...]
where the time goes in v5:
time: 126 us
  Pallas kernels  121 us (96%)
  local copies, waits for them, and re-layouts  4.82 us (4%)
    pallas_call x1, Pallas kernels, on_device(): pl.pallas_call(functools.partial(kernel, cfg), out_shape=(jax.ShapeDtypeS...  121 us

profile of v5, /device:TPU:1, one launch (start us, length us, event | category | flops | bytes accessed | tf_op | source)
XLA Modules:
  0.0 126.1 jit_solution(4917499782477962639)
XLA Ops:
  0.6 0.7 copy.17
  1.3 0.0 copy-start
  1.3 0.0 copy-start.1
  1.3 0.0 copy-start.2
  1.4 1.2 copy.8
  2.6 0.0 copy-start.3
  2.6 0.0 copy-done
  2.6 0.0 copy-done.1
  2.6 0.0 copy-done.2
  2.6 0.6 copy-done.3
  3.2 120.6 %shard_map.77 = (f32[4,128,256]{2,1,0:T(8,128)S(1)}, f32[4,128,256]{2,1,0:T(8,128)S(1)}) custom-call(s32[1,2]{1,0:T(1,128)S(1)} %copy-done.3, f32[4,128,256]{2,1,0:T(8,128)S(1)} %bitcast.17, f32[4,2,256]{2,1,0:T(2,128)S(1)} %bitcast.20, f32[4,64,256]{2,1,0:T(8,128)S(1)} %copy-done.2, bf16[2,256,256]{2,1,0:T(8,128)(2,1)S(1)} %copy-done.1, ...), custom_call_target="tpu_custom_call" | custom-call | tf_op jit(solution)/shard_map/pallas_call | solution.py:649
  123.8 1.1 copy.16
  125.0 1.1 copy.15
Async XLA Ops:
  1.3 1.3 copy-start
  1.3 1.3 %copy-start.1 = (bf16[2,256,256]{2,1,0:T(8,128)(2,1)S(1)}, bf16[2,256,256]{2,1,0:T(8,128)(2,1)}, u32[]{:S(2)}) copy-start(bf16[2,256,256]{2,1,0:T(8,128)(2,1)} %constant.7.clone.hy_ref) | copy-start | bytes 786436
  1.3 1.3 %copy-start.2 = (f32[4,64,256]{2,1,0:T(8,128)S(1)}, f32[4,64,256]{2,1,0:T(8,128)}, u32[]{:S(2)}) copy-start(f32[4,64,256]{2,1,0:T(8,128)} %constant.6.clone.tab_ref) | copy-start | bytes 786436
  2.6 0.7 copy-start.3

commit v6 on v5

--- a/solution.py
+++ b/solution.py
@@ -75,11 +75,11 @@
 
 def kernel(
     cfg,
-    pos_ref, chi0_ref, meas_ref, tab_ref, hy_ref, hz_ref,
-    w_ref, chi_out_ref,
-    chi1_ref, e_ref, s_ref, r_ref, d_ref, v_ref, b_ref, sp_all, rho_ref, early_ref, early_recv, late_ref, late_recv,
+    pos_ref, meas_ref, contrast_hbm, tab_hbm, hy_hbm, hz_hbm,
+    w_hbm, chi_hbm,
+    chi0_ref, tab_ref, hy_ref, hz_ref, w_ref, chi2_ref, chi1_ref, e_ref, s_ref, r_ref, d_ref, v_ref, b_ref, sp_all, rho_ref, early_ref, early_recv, late_ref, late_recv,
     send0_all, send1_all, send3_all, states_all, sums, recv1, recv2, recv3, recv4, red1, red2,
-    ex_send, ex_recv, red_send, red_recv, x_send, x_recv, late_send, late_took, chi_took,
+    ex_send, ex_recv, red_send, red_recv, x_send, x_recv, late_send, late_took, chi_took, local_sem,
 ):
     ns, g1, g2, nz, ny, rows = cfg
     halves = ny // 128
@@ -95,6 +95,15 @@
     base = grp * g1
 
     partner = (src, space + 1 - 2 * core)
+
+    for x in range(rows):
+        for c in range(2):
+            pltpu.make_async_copy(
+                contrast_hbm.at[c, :, x, :], chi0_ref.at[x, pl.ds(c * nz, nz), :], local_sem.at[0]
+            ).start()
+    pltpu.make_async_copy(hz_hbm, hz_ref, local_sem.at[1]).start()
+    pltpu.make_async_copy(hy_hbm, hy_ref, local_sem.at[2]).start()
+    pltpu.make_async_copy(tab_hbm, tab_ref, local_sem.at[3]).start()
 
     barrier = pltpu.get_barrier_semaphore()
 
@@ -408,7 +417,7 @@
     offset_y_sq = offset_y * offset_y
     level = lax.broadcasted_iota(jnp.int32, (8, ny), 0).astype(F32) + SOURCE_GAP
 
-    def begin(x, z, total):
+    def begin(x, z, carry):
         height = level + z.astype(F32)
         offset_x = (space * rows + x).astype(F32) - source_x
         dist = jnp.sqrt(height * height + offset_x * offset_x + offset_y_sq)
@@ -416,20 +425,28 @@
         sine, cosine = half_turn(turns - jnp.floor(turns + 0.5))
         wave = (1.0 - 2.0 * sine * sine, 2.0 * sine * cosine)
         put(e_ref, x, z, wave)
-        field = cmul(pair(chi0_ref, x, z), wave)
+        return carry
+
+    def excite(x, z, total):
+        field = cmul(pair(chi0_ref, x, z), pair(e_ref, x, z))
         put(w_ref, x, z, field)
         return total + square(field)
 
-    object_part = each_block(begin, zero)
+    each_block(begin, 0)
+    take(chi0_ref, local_sem.at[0])
+    object_part = each_block(excite, zero)
     data_part = jnp.zeros((1, ny), F32)
     for x in range(rows):
         for c in range(2):
-            data_part = data_part + meas_ref[x, pl.ds(c, 1), :] * meas_ref[x, pl.ds(c, 1), :]
+            data_part = data_part + meas_ref[c, pl.ds(x, 1), :] * meas_ref[c, pl.ds(x, 1), :]
     data_fold = data_part[:, :128]
     for h in range(1, halves):
         data_fold = data_fold + data_part[:, h * 128:(h + 1) * 128]
 
+    take(hz_ref, local_sem.at[1])
+    take(hy_ref, local_sem.at[2])
     local(w_ref, sp_all.at[0])
+    take(tab_ref, local_sem.at[3])
     pl.semaphore_wait(barrier, (g1 - 1) + (ns * g2 - 1))
     sweep_out(0)
     reduce_start(0, [data_fold, fold(object_part)])
@@ -449,7 +466,7 @@
         t = 1 + 2 * update
         a = 1 + 2 * update
         last = update == OUTER - 1
-        chi_next = chi_out_ref if last else chi1_ref
+        chi_next = chi2_ref if last else chi1_ref
         early, late = early_recv.at[update], late_recv.at[update]
         right, left, across = (lax.rem(src + k, ns) for k in (1, 3, 2))
 
@@ -479,7 +496,7 @@
                 remote(early_ref.at[x], early.at[k], x_send.at[update, 0], x_recv.at[update, 0], (x, space)).start()
         rho = jnp.concatenate(
             [
-                meas_ref[x, pl.ds(c, 1), :] - s_ref[x, pl.ds(c * nz, 1), :]
+                meas_ref[c, pl.ds(x, 1), :] - s_ref[x, pl.ds(c * nz, 1), :]
                 for x in range(rows) for c in range(2)
             ],
             axis=0,
@@ -488,8 +505,8 @@
 
         first, second = sp_all.at[t % 2], sp_all.at[(t + 1) % 2]
         local(v_ref, first)
-        local(b_ref, second)
         if update:
+            local(b_ref, second)
             object_share = float(ns) * reduce_end(2)[0:1] / data_total
 
         def rho_tile(i, part, c, object_share=object_share):
@@ -503,6 +520,8 @@
             return value[0] + ratio * rho_tile(i, part, 1), value[1] - ratio * rho_tile(i, part, 0)
 
         sweep_out(t, add_first)
+        if not update:
+            local(b_ref, second)
         sweep_out(t + 1, add_second)
         middle_out(t)
         middle_out(t + 1)
@@ -596,6 +615,12 @@
             return carry
 
         each_block(advance, 0)
+        if last:
+            for x in range(rows):
+                for c in range(2):
+                    pltpu.make_async_copy(
+                        w_ref.at[x, pl.ds(c * nz, nz), :], w_hbm.at[c, :, x, :], local_sem.at[4]
+                    ).start()
         for half in range(2):
             for place in (1, 2):
                 take(late.at[place, half], late_took.at[update, place, half])
@@ -616,22 +641,31 @@
             return total + square(chi)
 
         chi_part = lax.fori_loop(0, zgroups, contrast, zero, unroll=2)
+        if not last:
+            reduce_start(2, [fold(chi_part)])
         for k in (2, 1, 3):
             remote(chi_next.at[src], chi_next.at[src], x_send.at[update, 1], chi_took.at[update, k],
                    (lax.rem(src + k, ns), space)).start()
         if not last:
-            reduce_start(2, [fold(chi_part)])
             reduce_middle(2)
         else:
-            for k in range(1, ns):
-                take(chi_next.at[0], chi_took.at[update, k])
+            for k in (0, 1, 3, 2):
+                x = lax.rem(src + k, ns)
+                if k:
+                    take(chi_next.at[0], chi_took.at[update, ns - k])
+                for c in range(2):
+                    pltpu.make_async_copy(
+                        chi_next.at[x, pl.ds(c * nz, nz), :], chi_hbm.at[c, :, x, :], local_sem.at[5]
+                    ).start()
         take(early.at[pl.ds(1, ns - 1)], x_send.at[update, 0])
         for half in range(2):
             for place in range(3):
                 take(late.at[place, half], late_send.at[update, place, half])
         chi_ref = chi_next
     for update in range(OUTER):
-        take(chi_out_ref.at[pl.ds(0, ns - 1)], x_send.at[update, 1])
+        take(chi2_ref.at[pl.ds(0, ns - 1)], x_send.at[update, 1])
+    take(w_ref, local_sem.at[4])
+    take(chi2_ref, local_sem.at[5])
 
 
 def on_device(ns, g1, g2, contrast, measured, positions):
@@ -639,19 +673,23 @@
     cfg = (ns, g1, g2, nz, ny, rows)
     transforms = 1 + 2 * OUTER
     reductions = 2 * OUTER
-    chi0 = contrast.transpose(2, 0, 1, 3).reshape(rows, 2 * nz, ny)
-    meas = measured[0].transpose(1, 0, 2)
     tables = decay_tables(nz, ny)
     hy = high_low(hartley(ny))
     hz = high_low(np.kron(np.eye(4), hartley(nz)))
     field = (rows, 2 * nz, ny)
     vmem = pl.BlockSpec(memory_space=pltpu.VMEM)
+    anywhere = pl.BlockSpec(memory_space=pltpu.HBM)
     w, chi = pl.pallas_call(
         functools.partial(kernel, cfg),
-        out_shape=(jax.ShapeDtypeStruct(field, F32), jax.ShapeDtypeStruct(field, F32)),
-        in_specs=[pl.BlockSpec(memory_space=pltpu.SMEM)] + [vmem] * 5,
-        out_specs=(vmem, vmem),
-        scratch_shapes=[pltpu.VMEM(field, F32)] * 7 + [
+        out_shape=(jax.ShapeDtypeStruct(contrast.shape, F32), jax.ShapeDtypeStruct(contrast.shape, F32)),
+        in_specs=[pl.BlockSpec(memory_space=pltpu.SMEM), vmem] + [anywhere] * 4,
+        out_specs=(anywhere, anywhere),
+        scratch_shapes=[
+            pltpu.VMEM(field, F32),
+            pltpu.VMEM(tables.shape, F32),
+            pltpu.VMEM(hy.shape, BF16),
+            pltpu.VMEM(hz.shape, BF16),
+        ] + [pltpu.VMEM(field, F32)] * 9 + [
             pltpu.VMEM((2,) + field, F32),
             pltpu.VMEM((2 * rows, ny), F32),
             pltpu.VMEM((rows, 3 * nz, ny), F32),
@@ -678,13 +716,13 @@
             pltpu.SemaphoreType.DMA((OUTER, 3, 2)),
             pltpu.SemaphoreType.DMA((OUTER, 3, 2)),
             pltpu.SemaphoreType.DMA((OUTER, ns)),
+            pltpu.SemaphoreType.DMA((6,)),
         ],
         compiler_params=pltpu.CompilerParams(
-            collective_id=0, has_side_effects=True, vmem_limit_bytes=40 * 1024 * 1024
+            collective_id=0, has_side_effects=True, vmem_limit_bytes=56 * 1024 * 1024
         ),
-    )(positions, chi0, meas, tables, hy, hz)
-    sources = w.reshape(rows, 2, nz, ny).transpose(1, 2, 0, 3)[None]
-    return sources, chi.reshape(rows, 2, nz, ny).transpose(1, 2, 0, 3)
+    )(positions, measured[0], contrast, tables, hy, hz)
+    return w[None], chi
 
 
 def solution(mesh, g2=4):

time: 126 us -> 125 us (level)
  local copies, waits for them, and re-layouts: 4.82 us -> 2.72 us
    reshape x2 -> x0, local copies, waits for them, and re-layouts: 2.27 us -> none  [the longest x1 1.13 us: on_device(): sources = w.reshape(rows, 2, nz, ny).transpose(1, 2, 0, 3)[None]]
    unnamed x9 -> x4, local copies, waits for them, and re-layouts: 1.34 us -> 2.72 us
where the time goes in v6:
time: 125 us
  Pallas kernels  121 us (97%)
  local copies, waits for them, and re-layouts  2.72 us (2%)
    pallas_call x1, Pallas kernels, on_device(): pl.pallas_call(functools.partial(kernel, cfg), out_shape=(jax.ShapeDtypeS...  121 us
    unnamed x4, local copies, waits for them, and re-layouts  2.72 us

profile of v6, /device:TPU:1, one launch (start us, length us, event | category | flops | bytes accessed | tf_op | source)
XLA Modules:
  0.0 124.8 jit_solution(15168711178678364329)
XLA Ops:
  0.6 121.4 %shard_map.77 = (f32[2,64,4,256]{3,2,1,0:T(4,128)}, f32[2,64,4,256]{3,2,1,0:T(4,128)}) custom-call(s32[1,2]{1,0:T(1,128)} %pos_ref.1, f32[2,4,256]{2,1,0:T(4,128)} %bitcast.3, f32[2,64,4,256]{3,2,1,0:T(4,128)} %contrast_hbm.1, f32[4,64,256]{2,1,0:T(8,128)} %constant.6.clone.tab_hbm, bf16[2,256,256]{2,1,0:T(8,128)(2,1)} %constant.7.clone.hy_hbm, ...), custom_call_target="tpu_custom_call" | custom-call | tf_op jit(solution)/shard_map/pallas_call | solution.py:682
  122.1 0.0 copy-start
  122.1 1.9 %copy.10 = f32[1,2,64,4,256]{4,3,2,1,0:T(4,128)} copy(f32[1,2,64,4,256]{4,3,2,1,0:T(4,128)} %bitcast.2) | data formatting | bytes 1048576
  124.0 0.0 copy-done
  124.0 0.8 copy.11
Async XLA Ops:
  122.1 1.9 %copy-start = (f32[2,64,4,256]{3,2,1,0:T(4,128)S(1)}, f32[2,64,4,256]{3,2,1,0:T(4,128)}, u32[]{:S(2)}) copy-start(f32[2,64,4,256]{3,2,1,0:T(4,128)} %get-tuple-element.9) | copy-start | bytes 1572868

commit v7 on v6

--- a/solution.py
+++ b/solution.py
@@ -107,19 +107,32 @@
 
     barrier = pltpu.get_barrier_semaphore()
 
-    def greet_group(k, carry):
-        pl.semaphore_signal(barrier, inc=1, device_id=(src, base + lax.rem(m + k, g1)), device_id_type=MESH)
+    zs = g1 * g2 // 8
+    z_at, y_at = space // 8, lax.rem(space // 2, 4)
+
+    def column_peer(k):
+        return src, (lax.rem(z_at + k // 2, zs) * 4 + y_at) * 2 + lax.rem(core + k, 2)
+
+    def plane_peer(k):
+        return lax.rem(src + k // 4, ns), (z_at * 4 + lax.rem(y_at + k, 4)) * 2 + core
+
+    def greet_column(k, carry):
+        pl.semaphore_signal(barrier, inc=1, device_id=column_peer(k), device_id_type=MESH)
         return carry
 
-    def cross_peer(k):
-        return lax.rem(src + k // g2, ns), lax.rem(grp + lax.rem(k, g2), g2) * g1 + m
-
-    def greet_cross(k, carry):
-        pl.semaphore_signal(barrier, inc=1, device_id=cross_peer(k), device_id_type=MESH)
+    def greet_plane(k, carry):
+        pl.semaphore_signal(barrier, inc=1, device_id=plane_peer(k), device_id_type=MESH)
         return carry
 
-    lax.fori_loop(1, g1, greet_group, 0)
-    lax.fori_loop(1, ns * g2, greet_cross, 0)
+    def greet_diagonal(k, carry):
+        z_other = z_at + 1 - 2 * lax.rem(z_at, 2)
+        pl.semaphore_signal(barrier, inc=1, device_id=(src, (z_other * 4 + lax.rem(y_at + k, 4)) * 2 + core),
+                            device_id_type=MESH)
+        return carry
+
+    lax.fori_loop(1, 2 * zs, greet_column, 0)
+    lax.fori_loop(1, 4 * ns, greet_plane, 0)
+    lax.fori_loop(1, 4, greet_diagonal, 0)
 
     def remote(src_ref, dst_ref, send_sem, recv_sem, device):
         return pltpu.make_async_remote_copy(
@@ -133,38 +146,39 @@
     def reduce_start(a, parts):
         red1[a, 0] = jnp.concatenate(parts + [jnp.zeros((8 - len(parts), 128), F32)], axis=0)
 
-        def send(k, carry):
-            remote(red1.at[a, 0], red1.at[a, k], red_send.at[a, 0], red_recv.at[a, 0],
-                   (src, base + lax.rem(m + k, g1))).start()
-            return carry
-
-        lax.fori_loop(1, g1, send, 0)
+        def send(n, carry):
+            k = lax.rem(n + zs - 2, 2 * zs - 1) + 1
+            remote(red1.at[a, 0], red1.at[a, k], red_send.at[a, 0], red_recv.at[a, 0], column_peer(k)).start()
+            return carry
+
+        lax.fori_loop(1, 2 * zs, send, 0)
 
     def reduce_middle(a):
-        take(red1.at[a, pl.ds(1, g1 - 1)], red_recv.at[a, 0])
+        take(red1.at[a, pl.ds(1, 2 * zs - 1)], red_recv.at[a, 0])
 
         def add(j, total):
-            return total + red1[a, lax.rem(m - j + g1, g1)]
-
-        red2[a, 0] = lax.fori_loop(0, g1, add, jnp.zeros((8, 128), F32), unroll=True)
-        take(red1.at[a, pl.ds(1, g1 - 1)], red_send.at[a, 0])
-
-        def send(k, carry):
-            remote(red2.at[a, 0], red2.at[a, k], red_send.at[a, 1], red_recv.at[a, 1], cross_peer(k)).start()
-            return carry
-
-        lax.fori_loop(1, ns * g2, send, 0)
+            slot = lax.rem(z_at - j // 2 + zs, zs) * 2 + lax.rem(core + j, 2)
+            return total + red1[a, slot]
+
+        red2[a, 0] = lax.fori_loop(0, 2 * zs, add, jnp.zeros((8, 128), F32), unroll=True)
+
+        def send(n, carry):
+            k = lax.rem(n + 2 * ns, 4 * ns - 1) + 1
+            remote(red2.at[a, 0], red2.at[a, k], red_send.at[a, 1], red_recv.at[a, 1], plane_peer(k)).start()
+            return carry
+
+        lax.fori_loop(1, 4 * ns, send, 0)
+        take(red1.at[a, pl.ds(1, 2 * zs - 1)], red_send.at[a, 0])
 
     def reduce_end(a):
-        count = ns * g2
-        take(red2.at[a, pl.ds(1, count - 1)], red_recv.at[a, 1])
+        take(red2.at[a, pl.ds(1, 4 * ns - 1)], red_recv.at[a, 1])
 
         def add(j, total):
-            slot = lax.rem(src - j // g2 + ns, ns) * g2 + lax.rem(grp - lax.rem(j, g2) + g2, g2)
+            slot = lax.rem(src - j // 4 + ns, ns) * 4 + lax.rem(y_at - lax.rem(j, 4) + 4, 4)
             return total + red2[a, slot]
 
-        total = lax.fori_loop(0, count, add, jnp.zeros((8, 128), F32), unroll=True)
-        take(red2.at[a, pl.ds(1, count - 1)], red_send.at[a, 1])
+        total = lax.fori_loop(0, 4 * ns, add, jnp.zeros((8, 128), F32), unroll=True)
+        take(red2.at[a, pl.ds(1, 4 * ns - 1)], red_send.at[a, 1])
         return jnp.sum(total, axis=1, keepdims=True)
 
     def fold(acc):
@@ -294,7 +308,8 @@
             remote(recv2.at[t, 0], recv2.at[t, k], ex_send.at[t, 2], ex_recv.at[t, 2], (src, peer)).start()
             return carry
 
-        lax.fori_loop(1, g2, send, 0)
+        for k in (2, 1, 3):
+            send(k, 0)
 
     def middle_back(t):
         send3 = send3_all.at[t % 2]
@@ -447,7 +462,7 @@
     take(hy_ref, local_sem.at[2])
     local(w_ref, sp_all.at[0])
     take(tab_ref, local_sem.at[3])
-    pl.semaphore_wait(barrier, (g1 - 1) + (ns * g2 - 1))
+    pl.semaphore_wait(barrier, (2 * zs - 1) + (4 * ns - 1) + 3)
     sweep_out(0)
     reduce_start(0, [data_fold, fold(object_part)])
     middle_out(0)
@@ -705,8 +720,8 @@
             pltpu.VMEM((transforms, g2, 4, 8, 128), F32),
             pltpu.VMEM((transforms, g1 // 2, 4, 8, 128), F32),
             pltpu.VMEM((transforms, g1 // 2, 4, 8, 128), F32),
-            pltpu.VMEM((reductions, g1, 8, 128), F32),
-            pltpu.VMEM((reductions, ns * g2, 8, 128), F32),
+            pltpu.VMEM((reductions, g1 * g2 // 4, 8, 128), F32),
+            pltpu.VMEM((reductions, 4 * ns, 8, 128), F32),
             pltpu.SemaphoreType.DMA((transforms, 5)),
             pltpu.SemaphoreType.DMA((transforms, 5)),
             pltpu.SemaphoreType.DMA((reductions, 2)),

time: 125 us -> 123 us (0.984)
  Pallas kernels: 121 us -> 119 us
    pallas_call x1, Pallas kernels: 121 us -> 119 us  [on_device(): pl.pallas_call(functools.partial(kernel, cfg), out_shape=(jax.ShapeDtypeS...]
where the time goes in v7:
time: 123 us; the launch traced here: 122 us
  Pallas kernels  119 us (97%)
  local copies, waits for them, and re-layouts  2.72 us (2%)
    pallas_call x1, Pallas kernels, on_device(): pl.pallas_call(functools.partial(kernel, cfg), out_shape=(jax.ShapeDtypeS...  119 us
    unnamed x4, local copies, waits for them, and re-layouts  2.72 us

profile of v7, /device:TPU:1, one launch (start us, length us, event | category | flops | bytes accessed | tf_op | source)
XLA Modules:
  0.0 122.2 jit_solution(1505330527312115742)
XLA Ops:
  0.6 118.9 %shard_map.77 = (f32[2,64,4,256]{3,2,1,0:T(4,128)}, f32[2,64,4,256]{3,2,1,0:T(4,128)}) custom-call(s32[1,2]{1,0:T(1,128)} %pos_ref.1, f32[2,4,256]{2,1,0:T(4,128)} %bitcast.3, f32[2,64,4,256]{3,2,1,0:T(4,128)} %contrast_hbm.1, f32[4,64,256]{2,1,0:T(8,128)} %constant.6.clone.tab_hbm, bf16[2,256,256]{2,1,0:T(8,128)(2,1)} %constant.7.clone.hy_hbm, ...), custom_call_target="tpu_custom_call" | custom-call | tf_op jit(solution)/shard_map/pallas_call | solution.py:697
  119.5 0.0 copy-start
  119.5 1.9 %copy.10 = f32[1,2,64,4,256]{4,3,2,1,0:T(4,128)} copy(f32[1,2,64,4,256]{4,3,2,1,0:T(4,128)} %bitcast.2) | data formatting | bytes 1048576
  121.4 0.0 copy-done
  121.4 0.8 copy.11
Async XLA Ops:
  119.5 1.9 %copy-start = (f32[2,64,4,256]{3,2,1,0:T(4,128)S(1)}, f32[2,64,4,256]{3,2,1,0:T(4,128)}, u32[]{:S(2)}) copy-start(f32[2,64,4,256]{3,2,1,0:T(4,128)} %get-tuple-element.9) | copy-start | bytes 1572868

commit v8 on v7

--- a/solution.py
+++ b/solution.py
@@ -91,6 +91,7 @@
     chips = g1 // 2
     core = lax.rem(m, 2)
     chip = m // 2
+    far_first = (6, 2, 5, 3, 7, 1, 4)
     grp = space // g1
     base = grp * g1
 
@@ -195,14 +196,14 @@
         mm = functools.partial(jnp.dot, preferred_element_type=F32)
         return mm(a[0], b[0]) + (mm(a[1], b[0]) + mm(a[0], b[1]))
 
+    def local_pair(src_ref, dst_ref, n):
+        at = pl.ds(2 * n, 2)
+        depth_done = dot3((hz_ref[0], hz_ref[1]), split(src_ref[at].reshape(4 * nz, ny)))
+        dst_ref[at] = dot3(split(depth_done), (hy_ref[0], hy_ref[1])).reshape(2, 2 * nz, ny)
+
     def local(src_ref, dst_ref):
-        hz = (hz_ref[0], hz_ref[1])
-        hy = (hy_ref[0], hy_ref[1])
-        for pair in range(rows // 2):
-            block = src_ref[pl.ds(2 * pair, 2)].reshape(4 * nz, ny)
-            depth_done = dot3(hz, split(block))
-            done = dot3(split(depth_done), hy)
-            dst_ref[pl.ds(2 * pair, 2)] = done.reshape(2, 2 * nz, ny)
+        for n in range(rows // 2):
+            local_pair(src_ref, dst_ref, n)
 
     def tile(ref, lead, part, comp):
         z = pl.multiple_of(part // halves * 8, 8)
@@ -270,7 +271,8 @@
                    (src, base + 2 * g + core)).start()
             return carry
 
-        lax.fori_loop(1, chips, step, 0)
+        for k in far_first:
+            step(k, 0)
         vals = combine(chip)
         for c in range(4):
             recv1[t, 0, c] = vals[c]
@@ -348,7 +350,8 @@
                    (src, base + 2 * g + core)).start()
             return carry
 
-        lax.fori_loop(1, chips, send, 0)
+        for k in far_first:
+            send(k, 0)
         for c in range(4):
             recv3[t, 0, c] = send3[chip, c]
 
@@ -485,9 +488,12 @@
         early, late = early_recv.at[update], late_recv.at[update]
         right, left, across = (lax.rem(src + k, ns) for k in (1, 3, 2))
 
-        for k in (0, 3, 1, 2):
-            x = lax.rem(src + k, ns)
-            if update and k:
+        own_pair = src // 2
+        mate = src + 1 - 2 * lax.rem(src, 2)
+        first, second = sp_all.at[t % 2], sp_all.at[(t + 1) % 2]
+        for place, x in enumerate((src, mate, lax.rem(mate + 2, ns), across)):
+            k = lax.rem(x - src + ns, ns)
+            if update and place:
                 take(chi_ref.at[0], chi_took.at[update - 1, ns - k])
 
             def residual(n, carry, x=x, chi_ref=chi_ref):
@@ -507,8 +513,11 @@
                 return carry
 
             lax.fori_loop(0, zgroups, residual, 0, unroll=4)
-            if k:
+            if place:
                 remote(early_ref.at[x], early.at[k], x_send.at[update, 0], x_recv.at[update, 0], (x, space)).start()
+            if update and place == 1:
+                local_pair(v_ref, first, own_pair)
+                local_pair(b_ref, second, own_pair)
         rho = jnp.concatenate(
             [
                 meas_ref[c, pl.ds(x, 1), :] - s_ref[x, pl.ds(c * nz, 1), :]
@@ -518,10 +527,11 @@
         )
         rho_ref[...] = level_zero * dot3(split(rho), (hy_ref[0], hy_ref[1]))
 
-        first, second = sp_all.at[t % 2], sp_all.at[(t + 1) % 2]
-        local(v_ref, first)
-        if update:
-            local(b_ref, second)
+        if not update:
+            local(v_ref, first)
+        else:
+            local_pair(v_ref, first, 1 - own_pair)
+            local_pair(b_ref, second, 1 - own_pair)
             object_share = float(ns) * reduce_end(2)[0:1] / data_total
 
         def rho_tile(i, part, c, object_share=object_share):
@@ -545,9 +555,7 @@
         sweep_back(t)
         local(first, d_ref)
         sweep_back(t + 1)
-        local(second, v_ref)
-        finish(t)
-        finish(t + 1)
+        local_pair(second, v_ref, 1 - own_pair)
 
         def pass_late(row, half, place, device, update=update, late=late):
             remote(late_ref.at[row, half], late.at[place, half], late_send.at[update, place, half],
@@ -566,6 +574,8 @@
         totals = (zero, zero)
         for k in (2, 1, 3, 0):
             x = lax.rem(src + k, ns)
+            if k == 1:
+                local_pair(second, v_ref, own_pair)
 
             def descend(n, totals, x=x, chi_ref=chi_ref):
                 z = pl.multiple_of(n * 8, 8)
@@ -598,6 +608,8 @@
                 pass_late(right, 1, 1, right)
             elif k == 3:
                 pass_late(left, 0, 2, left)
+        finish(t)
+        finish(t + 1)
         image_part = jnp.zeros((1, ny), F32)
         for x in range(rows):
             image_part = image_part + square((v_ref[x, pl.ds(0, 1), :], v_ref[x, pl.ds(nz, 1), :]))
@@ -633,9 +645,8 @@
         if last:
             for x in range(rows):
                 for c in range(2):
-                    pltpu.make_async_copy(
-                        w_ref.at[x, pl.ds(c * nz, nz), :], w_hbm.at[c, :, x, :], local_sem.at[4]
-                    ).start()
+                    at = pl.ds(c * nz, nz)
+                    pltpu.make_async_copy(w_ref.at[x, at, :], w_hbm.at[x, at, :], local_sem.at[4]).start()
         for half in range(2):
             for place in (1, 2):
                 take(late.at[place, half], late_took.at[update, place, half])
@@ -669,9 +680,8 @@
                 if k:
                     take(chi_next.at[0], chi_took.at[update, ns - k])
                 for c in range(2):
-                    pltpu.make_async_copy(
-                        chi_next.at[x, pl.ds(c * nz, nz), :], chi_hbm.at[c, :, x, :], local_sem.at[5]
-                    ).start()
+                    at = pl.ds(c * nz, nz)
+                    pltpu.make_async_copy(chi_next.at[x, at, :], chi_hbm.at[x, at, :], local_sem.at[5]).start()
         take(early.at[pl.ds(1, ns - 1)], x_send.at[update, 0])
         for half in range(2):
             for place in range(3):
@@ -681,6 +691,16 @@
         take(chi2_ref.at[pl.ds(0, ns - 1)], x_send.at[update, 1])
     take(w_ref, local_sem.at[4])
     take(chi2_ref, local_sem.at[5])
+
+
+def unfold(w_ref, chi_ref, w_out, chi_out, sem):
+    for n, (src_ref, dst_ref) in enumerate(((w_ref, w_out), (chi_ref, chi_out))):
+        rows, nz = src_ref.shape[0], src_ref.shape[1] // 2
+        for x in range(rows):
+            for c in range(2):
+                pltpu.make_async_copy(src_ref.at[x, pl.ds(c * nz, nz), :], dst_ref.at[c, :, x, :], sem.at[n]).start()
+    pltpu.make_async_copy(w_ref, w_ref, sem.at[0]).wait()
+    pltpu.make_async_copy(chi_ref, chi_ref, sem.at[1]).wait()
 
 
 def on_device(ns, g1, g2, contrast, measured, positions):
@@ -696,7 +716,7 @@
     anywhere = pl.BlockSpec(memory_space=pltpu.HBM)
     w, chi = pl.pallas_call(
         functools.partial(kernel, cfg),
-        out_shape=(jax.ShapeDtypeStruct(contrast.shape, F32), jax.ShapeDtypeStruct(contrast.shape, F32)),
+        out_shape=(jax.ShapeDtypeStruct(field, F32), jax.ShapeDtypeStruct(field, F32)),
         in_specs=[pl.BlockSpec(memory_space=pltpu.SMEM), vmem] + [anywhere] * 4,
         out_specs=(anywhere, anywhere),
         scratch_shapes=[
@@ -737,6 +757,13 @@
             collective_id=0, has_side_effects=True, vmem_limit_bytes=56 * 1024 * 1024
         ),
     )(positions, measured[0], contrast, tables, hy, hz)
+    w, chi = pl.pallas_call(
+        unfold,
+        out_shape=(jax.ShapeDtypeStruct(contrast.shape, F32), jax.ShapeDtypeStruct(contrast.shape, F32)),
+        in_specs=[anywhere, anywhere],
+        out_specs=(anywhere, anywhere),
+        scratch_shapes=[pltpu.SemaphoreType.DMA((2,))],
+    )(w, chi)
     return w[None], chi
 
 

time: 123 us -> 152 us (1.24)
  Pallas kernels: 119 us -> 151 us
  local copies, waits for them, and re-layouts: 2.72 us -> 0 us
    pallas_call x0 -> x1, Pallas kernels: none -> 32.9 us  [on_device(): pl.pallas_call(unfold, out_shape=(jax.ShapeDtypeStruct(contrast.shape, F3...]
    unnamed x4 -> x0, local copies, waits for them, and re-layouts: 2.72 us -> none
where the time goes in v8:
time: 152 us; the launch traced here: 151 us
  Pallas kernels  151 us (99%)
    pallas_call x1, Pallas kernels, on_device(): pl.pallas_call(functools.partial(kernel, cfg), out_shape=(jax.ShapeDtypeS...  118 us
    pallas_call x1, Pallas kernels, on_device(): pl.pallas_call(unfold, out_shape=(jax.ShapeDtypeStruct(contrast.shape, F3...  32.9 us

profile of v8, /device:TPU:1, one launch (start us, length us, event | category | flops | bytes accessed | tf_op | source)
XLA Modules:
  0.0 151.4 jit_solution(6830723646911410288)
XLA Ops:
  0.6 117.9 %shard_map.77 = (f32[4,128,256]{2,1,0:T(8,128)}, f32[4,128,256]{2,1,0:T(8,128)}) custom-call(s32[1,2]{1,0:T(1,128)} %pos_ref.1, f32[2,4,256]{2,1,0:T(4,128)} %bitcast.2, f32[2,64,4,256]{3,2,1,0:T(4,128)} %contrast_hbm.1, f32[4,64,256]{2,1,0:T(8,128)} %constant.6.clone.tab_hbm, bf16[2,256,256]{2,1,0:T(8,128)(2,1)} %constant.7.clone.hy_hbm, ...), custom_call_target="tpu_custom_call" | custom-call | tf_op jit(solution)/shard_map/pallas_call | solution.py:717
  118.6 32.9 %shard_map.78 = (f32[2,64,4,256]{3,2,1,0:T(4,128)}, f32[2,64,4,256]{3,2,1,0:T(4,128)}) custom-call(f32[4,128,256]{2,1,0:T(8,128)} %get-tuple-element.6.w_ref, f32[4,128,256]{2,1,0:T(8,128)} %get-tuple-element.7.chi_ref), custom_call_target="tpu_custom_call" | custom-call | tf_op jit(solution)/shard_map/pallas_call | solution.py:760

commit v9 on v8

--- a/solution.py
+++ b/solution.py
@@ -760,9 +760,10 @@
     w, chi = pl.pallas_call(
         unfold,
         out_shape=(jax.ShapeDtypeStruct(contrast.shape, F32), jax.ShapeDtypeStruct(contrast.shape, F32)),
-        in_specs=[anywhere, anywhere],
+        in_specs=[vmem, vmem],
         out_specs=(anywhere, anywhere),
         scratch_shapes=[pltpu.SemaphoreType.DMA((2,))],
+        compiler_params=pltpu.CompilerParams(vmem_limit_bytes=56 * 1024 * 1024),
     )(w, chi)
     return w[None], chi
 

time: 152 us -> 121 us (0.80)
  Pallas kernels: 151 us -> 120 us
    pallas_call x1, Pallas kernels: 32.9 us -> 2.16 us  [on_device(): pl.pallas_call(unfold, out_shape=(jax.ShapeDtypeStruct(contrast.shape, F3...]
where the time goes in v9:
time: 121 us
  Pallas kernels  120 us (99%)
    pallas_call x1, Pallas kernels, on_device(): pl.pallas_call(functools.partial(kernel, cfg), out_shape=(jax.ShapeDtypeS...  118 us

profile of v9, /device:TPU:1, one launch (start us, length us, event | category | flops | bytes accessed | tf_op | source)
XLA Modules:
  0.0 120.7 jit_solution(9713683405081364056)
XLA Ops:
  0.6 117.9 %shard_map.77 = (f32[4,128,256]{2,1,0:T(8,128)}, f32[4,128,256]{2,1,0:T(8,128)}) custom-call(s32[1,2]{1,0:T(1,128)} %pos_ref.1, f32[2,4,256]{2,1,0:T(4,128)} %bitcast.2, f32[2,64,4,256]{3,2,1,0:T(4,128)} %contrast_hbm.1, f32[4,64,256]{2,1,0:T(8,128)} %constant.6.clone.tab_hbm, bf16[2,256,256]{2,1,0:T(8,128)(2,1)} %constant.7.clone.hy_hbm, ...), custom_call_target="tpu_custom_call" | custom-call | tf_op jit(solution)/shard_map/pallas_call | solution.py:717
  118.6 2.2 %shard_map.78 = (f32[2,64,4,256]{3,2,1,0:T(4,128)}, f32[2,64,4,256]{3,2,1,0:T(4,128)}) custom-call(f32[4,128,256]{2,1,0:T(8,128)} %get-tuple-element.6.w_ref, f32[4,128,256]{2,1,0:T(8,128)} %get-tuple-element.7.chi_ref), custom_call_target="tpu_custom_call" | custom-call | tf_op jit(solution)/shard_map/pallas_call | solution.py:760

commit v10 on v9

--- a/solution.py
+++ b/solution.py
@@ -252,8 +252,8 @@
                 sums[t, core, g, c] = vals[c]
             return carry
 
-        lax.fori_loop(1, chips + 1, other_half, 0, unroll=2)
-        lax.fori_loop(1, chips + 1, own_half, 0, unroll=2)
+        lax.fori_loop(1, chips + 1, other_half, 0, unroll=4)
+        lax.fori_loop(1, chips + 1, own_half, 0, unroll=4)
         take(sums.at[t, 1 - core], ex_recv.at[t, 0])
 
         def combine(g):
@@ -374,7 +374,7 @@
             remote(states.at[1 - core, g], recv4.at[t, g], ex_send.at[t, 4], ex_recv.at[t, 4], partner).start()
             return carry
 
-        lax.fori_loop(0, chips, pass_on, 0, unroll=2)
+        lax.fori_loop(0, chips, pass_on, 0, unroll=4)
 
         def apply(part, ends):
             root = ctable(part, 0)
@@ -401,9 +401,9 @@
             apply(2 * g + 1 - core, tuple(recv4[t, g, c] for c in range(4)))
             return carry
 
-        lax.fori_loop(0, chips, own_half, 0, unroll=2)
+        lax.fori_loop(0, chips, own_half, 0, unroll=4)
         take(recv4.at[t], ex_recv.at[t, 4])
-        lax.fori_loop(0, chips, other_half, 0, unroll=2)
+        lax.fori_loop(0, chips, other_half, 0, unroll=4)
 
     def finish(t):
         take(recv4.at[t], ex_send.at[t, 0])

time: 121 us -> 122 us (level)
  no operation moved by 1% of the time
where the time goes in v10:
time: 122 us
  Pallas kernels  121 us (99%)
    pallas_call x1, Pallas kernels, on_device(): pl.pallas_call(functools.partial(kernel, cfg), out_shape=(jax.ShapeDtypeS...  119 us

profile of v10, /device:TPU:1, one launch (start us, length us, event | category | flops | bytes accessed | tf_op | source)
XLA Modules:
  0.0 121.8 jit_solution(578966205798026444)
XLA Ops:
  0.6 119.0 %shard_map.77 = (f32[4,128,256]{2,1,0:T(8,128)}, f32[4,128,256]{2,1,0:T(8,128)}) custom-call(s32[1,2]{1,0:T(1,128)} %pos_ref.1, f32[2,4,256]{2,1,0:T(4,128)} %bitcast.2, f32[2,64,4,256]{3,2,1,0:T(4,128)} %contrast_hbm.1, f32[4,64,256]{2,1,0:T(8,128)} %constant.6.clone.tab_hbm, bf16[2,256,256]{2,1,0:T(8,128)(2,1)} %constant.7.clone.hy_hbm, ...), custom_call_target="tpu_custom_call" | custom-call | tf_op jit(solution)/shard_map/pallas_call | solution.py:717
  119.6 2.2 %shard_map.78 = (f32[2,64,4,256]{3,2,1,0:T(4,128)}, f32[2,64,4,256]{3,2,1,0:T(4,128)}) custom-call(f32[4,128,256]{2,1,0:T(8,128)} %get-tuple-element.6.w_ref, f32[4,128,256]{2,1,0:T(8,128)} %get-tuple-element.7.chi_ref), custom_call_target="tpu_custom_call" | custom-call | tf_op jit(solution)/shard_map/pallas_call | solution.py:760
